TPU v7x, 256 devices: a whole 4x4x8 slice. The times are simulated.
256 devices in a mesh: gx: 4 (over y), gy: 8 (over z), gz: 8 (over x, core).
Axes of the slice: x: 4, y: 4, z: 8, core: 2. Of those that a mesh axis runs over, the one named last changes fastest.
Arguments:
- populations: float32 [19, 16, 128, 1024], P(None, 'gx', 'gy', 'gz'), may hold values from 0.02 to 0.12
- solid: int32 [16, 128, 1024], P('gx', 'gy', 'gz'), may hold values 0 or 1
- coefficients: float32 [2048, 16, 256], P(('gx', 'gz')), may hold values from -0.09375 to 0.09375
- body_nodes: float32 [3, 512, 2048], P(None, 'gy', ('gx', 'gz')), may hold values from -2 to 2
- centers: float32 [3, 2048], P(None, ('gx', 'gz')), may hold values from -0.5 to 0.5
- angles: float32 [3, 2048], P(None, ('gx', 'gz')), may hold values from -3.140625 to 3.140625
- velocity: float32 [6, 2048], P(None, ('gx', 'gz')), may hold values from -0.5 to 0.5
- node_frac: float32 [3, 512, 2048], P(None, 'gy', ('gx', 'gz')), may hold values from 0 to 1
- node_cell: int32 [512, 2048], P('gy', ('gx', 'gz')), may hold values from 0 to 6014, as said below
- grain_tile: int32 [8, 2048, 1], P('gy', ('gx', 'gz')), may hold values from 0 to 31; in each aligned block of 64 rows (0 to 63, 64 to 127, ..., all dimensions but the last counted through in order) at most 4 rows name the same one
- send_grain: int32 [32, 128], P(('gx', 'gz')), may hold values from -1 to 63, as said below
- recv_partner: int32 [32, 128], P(('gx', 'gz')), may hold values from -1 to 63, as said below
Outputs:
- populations_out: float32 [19, 16, 128, 1024], P(None, 'gx', 'gy', 'gz')
- centers_out: float32 [3, 2048], P(None, ('gx', 'gz'))
- velocity_out: float32 [6, 2048], P(None, ('gx', 'gz'))
Inputs may be any that keep to these rules, and one draw needn't show every extreme that they name: `node_cell`: c = (x * 16 + y) * 128 + z with x < 3, y < 15, z < 127, so all eight corners lie in the tile. `grain_tile`: in the rows of one device at most 4 grains name the same tile, a bound that some block reaches. `send_grain`: -1 marks an empty slot; within each destination's 4 slots the live ones come first; slot k for destination d on source s is live exactly when slot k for source s on owner d is live in recv_partner; some owner receives all 4 slots live from every source. `recv_partner`: -1 marks an empty slot, matching send_grain as stated there.
All inputs are finite; a program needn't handle non-finite values. No bound on the sum of `solid` on one device may be relied on, other than what follows from the above.
Results may differ from a plain program's by a relative error of at most 0.0001.
Values sent between devices are 32-bit elements; how exact they have to be, the bound alone decides.
No kernel may reach another device: no remote copies, remote signals or barrier semaphores. Data moves between devices by JAX's collectives and lax.ppermute only.
A program may use at most 128 MiB of HBM per device.

v0:
```python
import functools

import jax
import jax.numpy as jnp
import numpy as np
from jax import lax
from jax.experimental import pallas as pl
from jax.experimental.pallas import tpu as pltpu
from jax.sharding import PartitionSpec as P

F32, BF16, I32 = jnp.float32, jnp.bfloat16, jnp.int32

DIRS = [
    (0, 0, 0),
    (1, 0, 0),
    (-1, 0, 0),
    (0, 1, 0),
    (0, -1, 0),
    (0, 0, 1),
    (0, 0, -1),
    (1, 1, 0),
    (-1, -1, 0),
    (1, -1, 0),
    (-1, 1, 0),
    (1, 0, 1),
    (-1, 0, -1),
    (1, 0, -1),
    (-1, 0, 1),
    (0, 1, 1),
    (0, -1, -1),
    (0, 1, -1),
    (0, -1, 1),
]
WEIGHTS = [float(np.float32(1.0 / 3.0))] + [float(np.float32(1.0 / 18.0))] * 6
WEIGHTS = WEIGHTS + [float(np.float32(1.0 / 36.0))] * 12
OPPOSITE = [0, 2, 1, 4, 3, 6, 5, 8, 7, 10, 9, 12, 11, 14, 13, 16, 15, 18, 17]
TAU = 0.9
STIFF = 0.5
CONTACT = 0.05
DT = 0.05
PLUS = [[q for q in range(19) if DIRS[q][axis] == 1] for axis in range(3)]
MINUS = [[q for q in range(19) if DIRS[q][axis] == -1] for axis in range(3)]


def iota(shape, dim):
    return lax.broadcasted_iota(I32, shape, dim)


def split2(x):
    high = x.astype(BF16)
    return high, (x - high.astype(F32)).astype(BF16)


def split3(x):
    high = x.astype(BF16)
    rest = x - high.astype(F32)
    middle = rest.astype(BF16)
    return high, middle, (rest - middle.astype(F32)).astype(BF16)


def dot(a, b):
    return lax.dot_general(a, b, (((1,), (0,)), ((), ())), preferred_element_type=F32)


def dot_nt(a, b):
    return lax.dot_general(a, b, (((1,), (1,)), ((), ())), preferred_element_type=F32)


def lanes_half():
    return iota((64, 128), 1) < 64


def slot_lane_ids():
    p = iota((64, 128), 0)
    return (p & 31) * 4 + (p >> 5) * 2 + (iota((64, 128), 1) >> 6)


def slot_onehot(row):
    p = iota((64, 128), 0)
    first = (p & 31) * 4 + (p >> 5) * 2
    lane = iota((64, 128), 1)
    col_a = jnp.sum(jnp.where(lane == first, row, 0.0), axis=1, keepdims=True)
    col_b = jnp.sum(jnp.where(lane == first + 1, row, 0.0), axis=1, keepdims=True)
    named = jnp.where(lanes_half(), col_a, col_b)
    return jnp.where(named == (lane & 63).astype(F32), 1.0, 0.0)


def tile_onehot(route2, route_col):
    lane = iota((64, 128), 1)
    same = (route2 == route_col) & (iota((64, 128), 0) < (lane & 63))
    rank = jnp.sum(jnp.where(same, 1.0, 0.0), axis=0, keepdims=True)
    slot = route2 * 4.0 + rank
    return jnp.where(slot == slot_lane_ids().astype(F32), 1.0, 0.0)


def field(state, f):
    return jnp.where(lanes_half(), state[:, f : f + 1], state[:, 64 + f : 65 + f])


def strided(ref, count, stride, first):
    return jnp.concatenate(
        [ref[pl.ds(first + h, count, stride=stride), :] for h in range(2)], axis=0
    )


def store_strided(ref, value, stride, first):
    for h in range(2):
        ref[pl.ds(first + h, 32, stride=stride), :] = value[h * 32 : (h + 1) * 32]


def cross(a, b):
    return [
        a[1] * b[2] - a[2] * b[1],
        a[2] * b[0] - a[0] * b[2],
        a[0] * b[1] - a[1] * b[0],
    ]


def lane_sums(values, firsts):
    lane = iota((64, 128), 1)
    half = lanes_half()
    out = jnp.zeros((64, 128), F32)
    for value, first in zip(values, firsts):
        sum_a = jnp.sum(jnp.where(half, value, 0.0), axis=1, keepdims=True)
        sum_b = jnp.sum(jnp.where(half, 0.0, value), axis=1, keepdims=True)
        out = jnp.where(lane == first, sum_a, out)
        out = jnp.where(lane == 64 + first, sum_b, out)
    return out


def pack_kernel(
    body, frac, cell, centers, angles, velocity, send, route2, route_col, out, state, spread
):
    ca, sa = jnp.cos(angles[0:1, :]), jnp.sin(angles[0:1, :])
    cb, sb = jnp.cos(angles[1:2, :]), jnp.sin(angles[1:2, :])
    cc, sc = jnp.cos(angles[2:3, :]), jnp.sin(angles[2:3, :])
    rows = [
        cc * cb,
        cc * sb * sa - sc * ca,
        cc * sb * ca + sc * sa,
        sc * cb,
        sc * sb * sa + cc * ca,
        sc * sb * ca - cc * sa,
        -sb,
        cb * sa,
        cb * ca,
    ]
    state[...] = jnp.zeros((24, 64), F32)
    for i, row in enumerate(rows):
        state[i : i + 1, :] = row
    state[9:12, :] = centers[...]
    state[12:18, :] = velocity[...]
    spread[...] = jnp.zeros((1024, 128), F32)
    for c in range(8):
        if c < 3:
            value = body[c]
        elif c < 6:
            value = frac[c - 3]
        elif c == 6:
            value = (cell[...] + 1).astype(F32)
        else:
            value = state[...]
        count = value.shape[0]
        for h in range(2):
            first = c * 128 + h * 64
            spread[first : first + count, h * 64 : h * 64 + 64] = value
    tile_hot = tile_onehot(route2[...], route_col[...]).astype(BF16)
    pair_hot = slot_onehot(send[...]).astype(BF16)
    for c in range(8):
        parts = split3(spread[c * 128 : (c + 1) * 128, :])
        picked = dot_nt(tile_hot, parts[2]) + dot_nt(tile_hot, parts[1])
        store_strided(out, picked + dot_nt(tile_hot, parts[0]), 24, 2 * c)
        if c < 3 or c == 7:
            picked = dot_nt(pair_hot, parts[2]) + dot_nt(pair_hot, parts[1])
            picked = picked + dot_nt(pair_hot, parts[0])
            store_strided(out, picked, 24, 16 + 2 * min(c, 3))


def table_kernel(coefs, out):
    parts = split3(coefs[...].reshape(1024, 256))
    source = iota((256, 256), 0)
    lane = iota((256, 256), 1)
    within = lane & 127
    ranges = ((0, 48), (48, 80), (80, 96))
    for b in range(0, 16, 2):
        wanted = (b + (lane >> 7)) * 16 + (within & 15)
        total = None
        for part, (low, high) in zip(parts, ranges):
            pick = (source == wanted) & (within >= low) & (within < high)
            term = dot(part, jnp.where(pick, 1.0, 0.0).astype(BF16))
            total = term if total is None else total + term
        total = total.astype(BF16)
        for k in range(2):
            piece = total[:, k * 128 : (k + 1) * 128].reshape(64, 16, 128)
            out[:, (b + k) * 16 : (b + k + 1) * 16, :] = piece


def contact_kernel(
    own_first,
    partner_first,
    partner_stride,
    partners,
    bodies,
    partner_state,
    state,
    recv_row,
    hydro,
    table,
    payload,
    local,
    zt,
    zs,
    yt,
    ys,
    xt,
    xs,
    found,
):
    pst = strided(partner_state, 32, partner_stride, partner_first)
    body = [strided(bodies, 32, 24, 16 + 2 * c) for c in range(3)]
    hold_hot = slot_onehot(recv_row[...])
    own = jnp.concatenate([state[...], jnp.zeros((40, 64), F32)], axis=0)
    parts = split3(own)
    hot_a = hold_hot[:, :64].astype(BF16)
    hot_b = hold_hot[:, 64:].astype(BF16)
    own_a = dot_nt(hot_a, parts[2]) + dot_nt(hot_a, parts[1]) + dot_nt(hot_a, parts[0])
    own_b = dot_nt(hot_b, parts[2]) + dot_nt(hot_b, parts[1]) + dot_nt(hot_b, parts[0])
    half = lanes_half()

    def held(f):
        return jnp.where(half, own_a[:, f : f + 1], own_b[:, f : f + 1])

    arm = []
    for i in range(3):
        arm.append(
            field(pst, 3 * i) * body[0]
            + field(pst, 3 * i + 1) * body[1]
            + field(pst, 3 * i + 2) * body[2]
        )
    rel = [arm[i] + (field(pst, 9 + i) - held(9 + i)) for i in range(3)]
    rot = [[held(3 * i + j) for j in range(3)] for i in range(3)]
    for axis, (kinds, slopes) in enumerate(((xt, xs), (yt, ys), (zt, zs))):
        y = rot[0][axis] * rel[0] + rot[1][axis] * rel[1] + rot[2][axis] * rel[2]
        y = jnp.clip(y, -1.0, 1.0)
        twice = 2.0 * y
        t_old, t_new = jnp.ones((64, 128), F32), y
        u_old, u_new = jnp.zeros((64, 128), F32), jnp.ones((64, 128), F32)
        kinds[pl.ds(0, 64, stride=16), :] = t_old
        slopes[pl.ds(0, 64, stride=16), :] = u_old
        for n in range(1, 16):
            kinds[pl.ds(n, 64, stride=16), :] = t_new
            slopes[pl.ds(n, 64, stride=16), :] = float(n) * u_new
            t_old, t_new = t_new, twice * t_new - t_old
            u_old, u_new = u_new, twice * u_new - u_old
    low = iota((16, 128), 1) < 64
    zero = jnp.zeros((16, 256), BF16)

    def one(p):
        slot = (p & 31) * 4 + (p >> 5) * 2
        grain_a = jnp.maximum(partners[0, slot], 0)
        grain_b = jnp.maximum(partners[0, slot + 1], 0)
        left = jnp.concatenate([table[grain_a], table[grain_b]], axis=1)
        at = pl.ds(pl.multiple_of(p * 16, 16), 16)
        z_value, z_slope = zt[at, :], zs[at, :]
        blocks = []
        for keep in (low, jnp.logical_not(low)):
            value = split3(jnp.where(keep, z_value, 0.0))
            slope = split3(jnp.where(keep, z_slope, 0.0))
            both = [jnp.concatenate([value[i], slope[i]], axis=1) for i in range(3)]
            blocks += [both[0], both[1], both[2], both[0], both[1], both[0], zero, zero]
        right = jnp.concatenate(blocks, axis=0)
        sums = dot(left, right)
        y_kind, y_slope = yt[at, :], ys[at, :]
        value = jnp.zeros((16, 128), F32)
        value_y = jnp.zeros((16, 128), F32)
        value_z = jnp.zeros((16, 128), F32)
        for b in range(16):
            plain = sums[b * 16 : (b + 1) * 16, :128]
            steep = sums[b * 16 : (b + 1) * 16, 128:]
            value = value + plain * y_kind[b : b + 1]
            value_y = value_y + plain * y_slope[b : b + 1]
            value_z = value_z + steep * y_kind[b : b + 1]
        x_kind, x_slope = xt[at, :], xs[at, :]
        for i, term in enumerate(
            (value * x_kind, value * x_slope, value_y * x_kind, value_z * x_kind)
        ):
            found[i, pl.ds(p, 1), :] = jnp.sum(term, axis=0, keepdims=True)

    def two(i, carry):
        one(2 * i)
        one(2 * i + 1)
        return carry

    lax.fori_loop(0, 32, two, 0)
    level = found[0]
    grad = [found[1], found[2], found[3]]
    alive = jnp.sum(hold_hot.reshape(64, 128) * jnp.where(half, 1.0, 0.0), axis=1, keepdims=True)
    alive_b = jnp.sum(hold_hot * jnp.where(half, 0.0, 1.0), axis=1, keepdims=True)
    alive = jnp.where(half, alive, alive_b)
    norm = 1.0 + grad[0] * grad[0] + grad[1] * grad[1] + grad[2] * grad[2]
    strength = alive * (CONTACT * jnp.maximum(-level, 0.0) / jnp.sqrt(norm))
    force = [
        (rot[i][0] * grad[0] + rot[i][1] * grad[1] + rot[i][2] * grad[2]) * strength
        for i in range(3)
    ]
    on_holder = cross(rel, force)
    on_partner = cross(arm, force)
    summed = lane_sums(force + on_partner + on_holder, [0, 1, 2, 3, 4, 5, 18, 19, 20])
    lane = iota((64, 128), 1) & 63
    store_strided(payload, jnp.where(lane < 6, summed, hydro[...]), 2, 0)
    local[...] = summed


def node_setup(recv, refs):
    fx, fy, fz, base, alive = refs
    fx[...] = strided(recv, 32, 24, 6)
    fy[...] = strided(recv, 32, 24, 8)
    fz[...] = strided(recv, 32, 24, 10)
    named = strided(recv, 32, 24, 12)
    base[...] = jnp.maximum(named.astype(I32) - 1, 0)
    alive[...] = jnp.where(named > 0.5, 1.0, 0.0)


def node_weights(refs, p):
    fx, fy, fz, base, _ = refs
    at = pl.ds(p, 1)
    cell = base[at, :]
    x, y, z = cell >> 11, (cell >> 7) & 15, cell & 127
    gap = iota((128, 128), 0) - z
    up = fz[at, :]
    along_z = jnp.where(gap == 0, 1.0 - up, jnp.where(gap == 1, up, 0.0))
    gap = iota((16, 128), 0) - y
    up = fy[at, :]
    along_y = jnp.where(gap == 0, 1.0 - up, jnp.where(gap == 1, up, 0.0))
    up = fx[at, :]
    both = []
    for cx in range(4):
        weight = jnp.where(x == cx, 1.0 - up, jnp.where(x == cx - 1, up, 0.0))
        both.append(weight * along_y)
    return split2(along_z), jnp.concatenate(both, axis=0)


def pair_weights(refs, i):
    first, second = node_weights(refs, 2 * i), node_weights(refs, 2 * i + 1)
    high = jnp.concatenate([first[0][0], second[0][0]], axis=1)
    low = jnp.concatenate([first[0][1], second[0][1]], axis=1)
    return high, low, jnp.concatenate([first[1], second[1]], axis=1)


def moments(get):
    density = None
    flow = [None, None, None]
    for q in range(19):
        value = get(q)
        density = value if density is None else density + value
        for axis in range(3):
            if DIRS[q][axis] == 0:
                continue
            if flow[axis] is None:
                flow[axis] = value if DIRS[q][axis] > 0 else -value
            elif DIRS[q][axis] > 0:
                flow[axis] = flow[axis] + value
            else:
                flow[axis] = flow[axis] - value
    return density, [f / density for f in flow]


def flow_operand(flow, operand):
    for axis in range(3):
        high, low = split2(flow[axis])
        rows = slice(axis * 64, axis * 64 + 64)
        operand[rows, 0:128] = high
        operand[rows, 128:256] = high
        operand[rows, 256:384] = low


def interpolate(operand, high, low, across):
    along = dot(operand[...], jnp.concatenate([high, low, high], axis=0))
    return [
        jnp.sum(along[c * 64 : (c + 1) * 64] * across, axis=0, keepdims=True) for c in range(3)
    ]


def spread_pair(total, force, high, low, across):
    push = jnp.concatenate([force[c] * across for c in range(3)], axis=0)
    push_high, push_low = split2(push)
    total[...] += dot_nt(
        jnp.concatenate([push_high, push_low], axis=0), jnp.concatenate([high, low], axis=0)
    )


def node_speed(recv, state):
    body = [strided(recv, 32, 24, 2 * c) for c in range(3)]
    arm = [
        field(state, 3 * i) * body[0]
        + field(state, 3 * i + 1) * body[1]
        + field(state, 3 * i + 2) * body[2]
        for i in range(3)
    ]
    spin = [field(state, 15 + i) for i in range(3)]
    turned = cross(spin, arm)
    return [field(state, 12 + i) + turned[i] for i in range(3)]


def hydro_sums(recv, interp):
    body = [strided(recv, 32, 24, 2 * c) for c in range(3)]
    values = [interp[c] for c in range(3)]
    values += [body[j] * interp[k] for j in range(3) for k in range(3)]
    return lane_sums(values, list(range(6, 18)))


def collide(get, density, flow, total, solid, post, y_up, y_down):
    wall = solid[...].reshape(64, 128) > 0
    scale = TAU / density
    moved = []
    for c in range(3):
        rows = slice(c * 64, (c + 1) * 64)
        lows = slice(192 + c * 64, 192 + (c + 1) * 64)
        push = total[rows, 0:128] + (total[rows, 128:256] + total[lows, 0:128])
        moved.append(flow[c] + scale * push)
    speed = moved[0] * moved[0] + moved[1] * moved[1] + moved[2] * moved[2]
    base = 1.0 - 1.5 * speed
    for q in range(19):
        along = None
        for axis in range(3):
            if DIRS[q][axis] == 0:
                continue
            term = moved[axis] if DIRS[q][axis] > 0 else -moved[axis]
            along = term if along is None else along + term
        bracket = base if along is None else base + along * (3.0 + 4.5 * along)
        value = get(q)
        relaxed = value - (value - WEIGHTS[q] * density * bracket) * (1.0 / TAU)
        post[q] = jnp.where(wall, value, relaxed)
    for i in range(5):
        for x in range(4):
            row = i * 4 + x
            y_up[row : row + 1, :] = post[PLUS[1][i], x * 16 + 15 : x * 16 + 16, :]
            y_down[row : row + 1, :] = post[MINUS[1][i], x * 16 : x * 16 + 1, :]


def first_fluid_kernel(
    recv, fluid, solid, post, y_up, y_down, hydro, operand, total, interp, speeds, *refs
):
    get = lambda q: fluid[q].reshape(64, 128)
    density, flow = moments(get)
    flow_operand(flow, operand)
    node_setup(recv, refs)
    speed = node_speed(recv, strided(recv, 32, 24, 14))
    for c in range(3):
        speeds[c] = speed[c]
    total[...] = jnp.zeros((384, 256), F32)
    alive = refs[4]

    def pair(i, carry):
        high, low, across = pair_weights(refs, i)
        found = interpolate(operand, high, low, across)
        force = []
        for c in range(3):
            sides = []
            for k in range(2):
                at = pl.ds(2 * i + k, 1)
                side = found[c][:, k * 128 : (k + 1) * 128]
                interp[c, at, :] = side
                sides.append(STIFF * (speeds[c, at, :] - side) * alive[at, :])
            force.append(jnp.concatenate(sides, axis=1))
        spread_pair(total, force, high, low, across)
        return carry

    lax.fori_loop(0, 32, pair, 0)
    hydro[...] = hydro_sums(recv, interp)
    collide(get, density, flow, total, solid, post, y_up, y_down)


def shifted_y(post, q, x, y_low, y_high):
    value = post[q, x * 16 : (x + 1) * 16, :]
    step = DIRS[q][1]
    if step == 0:
        return value
    row = iota((16, 128), 0)
    if step > 0:
        at = PLUS[1].index(q) * 4 + x
        return jnp.where(row == 0, y_low[at : at + 1, :], pltpu.roll(value, 1, 0))
    at = MINUS[1].index(q) * 4 + x
    return jnp.where(row == 15, y_high[at : at + 1, :], pltpu.roll(value, 15, 0))


def shifted_yx(post, q, x, y_low, y_high, x_low, x_high):
    source = x - DIRS[q][0]
    if source < 0:
        at = PLUS[0].index(q) * 16
        return x_low[at : at + 16, :]
    if source > 3:
        at = MINUS[0].index(q) * 16
        return x_high[at : at + 16, :]
    return shifted_y(post, q, source, y_low, y_high)


def faces_x_kernel(post, y_low, y_high, x_up, x_down):
    for i in range(5):
        rows = slice(i * 16, (i + 1) * 16)
        x_up[rows, :] = shifted_y(post, PLUS[0][i], 3, y_low, y_high)
        x_down[rows, :] = shifted_y(post, MINUS[0][i], 0, y_low, y_high)


def faces_z_kernel(post, y_low, y_high, x_low, x_high, z_up, z_down):
    lane = iota((16, 128), 1)
    up = jnp.zeros((16, 128), F32)
    down = jnp.zeros((16, 128), F32)
    for i in range(5):
        for x in range(4):
            value = shifted_yx(post, PLUS[2][i], x, y_low, y_high, x_low, x_high)
            up = jnp.where(lane == i * 4 + x, value[:, 127:128], up)
            value = shifted_yx(post, MINUS[2][i], x, y_low, y_high, x_low, x_high)
            down = jnp.where(lane == i * 4 + x, value[:, 0:1], down)
    z_up[...] = up
    z_down[...] = down


def stream(post, solid, halos, out):
    y_low, y_high, x_low, x_high, z_low, z_high = halos
    lane = iota((16, 128), 1)

    def moved(q, x):
        value = shifted_yx(post, q, x, y_low, y_high, x_low, x_high)
        step = DIRS[q][2]
        if step == 0:
            return value
        if step > 0:
            at = PLUS[2].index(q) * 4 + x
            return jnp.where(lane == 0, z_low[:, at : at + 1], pltpu.roll(value, 1, 1))
        at = MINUS[2].index(q) * 4 + x
        return jnp.where(lane == 127, z_high[:, at : at + 1], pltpu.roll(value, 127, 1))

    for x in range(4):
        wall = solid[x] > 0
        for q in range(19):
            other = OPPOSITE[q]
            if other < q:
                continue
            value = moved(q, x)
            if other == q:
                out[q, x] = value
                continue
            back = moved(other, x)
            out[q, x] = jnp.where(wall, back, value)
            out[other, x] = jnp.where(wall, value, back)


def stream_kernel(post, solid, *refs):
    stream(post, solid, refs[:6], refs[6])


def stream_interp_kernel(post, solid, recv, *refs):
    halos = refs[:6]
    fluid, hydro, interp, operand = refs[6:10]
    scratch = refs[10:]
    stream(post, solid, halos, fluid)
    _, flow = moments(lambda q: fluid[q].reshape(64, 128))
    flow_operand(flow, operand)
    node_setup(recv, scratch)

    def pair(i, carry):
        high, low, across = pair_weights(scratch, i)
        found = interpolate(operand, high, low, across)
        for c in range(3):
            for k in range(2):
                at = pl.ds(2 * i + k, 1)
                interp[c, at, :] = found[c][:, k * 128 : (k + 1) * 128]
        return carry

    lax.fori_loop(0, 32, pair, 0)
    hydro[...] = hydro_sums(recv, interp)


def second_fluid_kernel(
    recv, states, fluid, solid, interp, post, y_up, y_down, total, speeds, *refs
):
    get = lambda q: fluid[q].reshape(64, 128)
    density, flow = moments(get)
    node_setup(recv, refs)
    alive = refs[4]
    speed = node_speed(recv, strided(states, 32, 4, 2))
    for c in range(3):
        speeds[c] = STIFF * (speed[c] - interp[c]) * alive[...]
    total[...] = jnp.zeros((384, 256), F32)

    def pair(i, carry):
        high, low, across = pair_weights(refs, i)
        force = [
            jnp.concatenate([speeds[c, pl.ds(2 * i + k, 1), :] for k in range(2)], axis=1)
            for c in range(3)
        ]
        spread_pair(total, force, high, low, across)
        return carry

    lax.fori_loop(0, 32, pair, 0)
    collide(get, density, flow, total, solid, post, y_up, y_down)


def by_grain(value, hot):
    turned = jnp.transpose(jnp.concatenate([value, jnp.zeros((64, 128), F32)], axis=0))
    out = None
    for h in range(2):
        for part in split3(turned[h * 64 : (h + 1) * 64, 0:64]):
            term = dot(part, hot[:, h * 64 : (h + 1) * 64].astype(BF16))
            out = term if out is None else out + term
    return out


def rotation_rows(state):
    return [[state[3 * i + j : 3 * i + j + 1, :] for j in range(3)] for i in range(3)]


def matmul3(a, b):
    return [
        [a[i][0] * b[0][k] + a[i][1] * b[1][k] + a[i][2] * b[2][k] for k in range(3)]
        for i in range(3)
    ]


def spin_matrix(w):
    zero = jnp.zeros_like(w[0])
    return [[zero, -w[2], w[1]], [w[2], zero, -w[0]], [-w[1], w[0], zero]]


def loads_kernel(back, local, state, body, send, recv_row, route2, route_col, out):
    returned = strided(back, 32, 2, 0)
    on_partner = by_grain(returned, slot_onehot(send[...]))
    fluid_sums = by_grain(returned, tile_onehot(route2[...], route_col[...]))
    on_holder = by_grain(local[...], slot_onehot(recv_row[...]))
    state = state[...]
    rot = rotation_rows(state)
    velocity = [state[12 + i : 13 + i, :] for i in range(3)]
    spin = [state[15 + i : 16 + i, :] for i in range(3)]
    turn = matmul3(spin_matrix(spin), rot)
    nodes = [body[c] for c in range(3)]
    first = [jnp.sum(nodes[c], axis=0, keepdims=True) for c in range(3)]
    pairs = [[None] * 3 for _ in range(3)]
    for i in range(3):
        for j in range(i, 3):
            pairs[i][j] = jnp.sum(nodes[i] * nodes[j], axis=0, keepdims=True)
            pairs[j][i] = pairs[i][j]
    interp = [fluid_sums[6 + c : 7 + c, :] for c in range(3)]
    mixed = [[fluid_sums[9 + 3 * j + k : 10 + 3 * j + k, :] for k in range(3)] for j in range(3)]
    count = float(body.shape[1])
    transposed = [[turn[j][i] for j in range(3)] for i in range(3)]
    arm = [rot[i][0] * first[0] + rot[i][1] * first[1] + rot[i][2] * first[2] for i in range(3)]
    carried = [turn[i][0] * first[0] + turn[i][1] * first[1] + turn[i][2] * first[2] for i in range(3)]
    outer = matmul3(rot, matmul3(pairs, transposed))
    drag = matmul3(rot, mixed)
    lever = cross(arm, velocity)
    out8 = []
    for i in range(3):
        force = count * velocity[i] + carried[i] - interp[i]
        total = on_partner[i : i + 1] - on_holder[i : i + 1] - STIFF * force
        out8.append(total)
    for i in range(3):
        j, k = (i + 1) % 3, (i + 2) % 3
        force = lever[i] + (outer[j][k] - outer[k][j]) - (drag[j][k] - drag[k][j])
        total = on_partner[3 + i : 4 + i] - on_holder[18 + i : 19 + i] - STIFF * force
        out8.append(total)
    for row, value in enumerate(out8):
        for copy in range(8):
            out[copy * 8 + row : copy * 8 + row + 1, 0:64] = value


def advance(totals, state):
    total = totals[0:8, 0:64]
    for copy in range(1, 8):
        total = total + totals[copy * 8 : copy * 8 + 8, 0:64]
    state = state[...]
    motion = [state[12 + i : 13 + i, :] + DT * total[i : i + 1, :] for i in range(6)]
    centre = [state[9 + i : 10 + i, :] + DT * motion[i] for i in range(3)]
    rot = rotation_rows(state)
    change = matmul3(spin_matrix(motion[3:6]), rot)
    rows = [rot[i][j] + DT * change[i][j] for i in range(3) for j in range(3)]
    return rows + centre + motion


def middle_kernel(totals, state, send, route2, route_col, out, fresh, spread):
    fresh[...] = jnp.zeros((24, 64), F32)
    for i, row in enumerate(advance(totals, state)):
        fresh[i : i + 1, :] = row
    spread[...] = jnp.zeros((128, 128), F32)
    spread[0:24, 0:64] = fresh[...]
    spread[64:88, 64:128] = fresh[...]
    parts = split3(spread[...])
    hots = (slot_onehot(send[...]), tile_onehot(route2[...], route_col[...]))
    for at, hot in enumerate(hots):
        hot = hot.astype(BF16)
        picked = dot_nt(hot, parts[2]) + dot_nt(hot, parts[1]) + dot_nt(hot, parts[0])
        store_strided(out, picked, 4, 2 * at)


def last_kernel(totals, state, centre, motion):
    rows = advance(totals, state)
    for i in range(3):
        centre[i : i + 1, :] = rows[9 + i]
    for i in range(6):
        motion[i : i + 1, :] = rows[12 + i]


VMEM = pl.BlockSpec(memory_space=pltpu.VMEM)
SMEM = pl.BlockSpec(memory_space=pltpu.SMEM)


def call(kernel, outs, args, scratch=(), scalars=0, name=None):
    shapes = [jax.ShapeDtypeStruct(shape, dtype) for shape, dtype in outs]
    return pl.pallas_call(
        kernel,
        out_shape=shapes,
        in_specs=[SMEM] * scalars + [VMEM] * (len(args) - scalars),
        out_specs=[VMEM] * len(outs),
        scratch_shapes=list(scratch),
        name=name,
    )(*args)


def scratch(*shape, dtype=F32):
    return pltpu.VMEM(shape, dtype)


def exchange(value, axes, parts):
    rows, lanes = value.shape
    out = lax.all_to_all(
        value.reshape(parts, rows // parts, lanes), axes, split_axis=0, concat_axis=0, tiled=True
    )
    return out.reshape(rows, lanes)


def neighbours(up, down, axis):
    n = lax.axis_size(axis)
    forward = [(i, (i + 1) % n) for i in range(n)]
    backward = [((i + 1) % n, i) for i in range(n)]
    return lax.ppermute(up, axis, forward), lax.ppermute(down, axis, backward)


def per_device(
    populations,
    solid,
    coefficients,
    body_nodes,
    centers,
    angles,
    velocity,
    node_frac,
    node_cell,
    grain_tile,
    send_grain,
    recv_partner,
):
    across = ("gx", "gz")
    send = send_grain.astype(F32)
    recv_row = recv_partner.astype(F32)
    route_col = grain_tile.reshape(64, 1).astype(F32)
    route = route_col.reshape(1, 64)
    route2 = jnp.concatenate([route, route], axis=1)
    packed, state = call(
        pack_kernel,
        [((768, 128), F32), ((24, 64), F32)],
        [body_nodes, node_frac, node_cell, centers, angles, velocity, send, route2, route_col],
        [scratch(1024, 128)],
        name="pack",
    )
    recv = exchange(packed, across, 32)
    table = call(table_kernel, [((64, 256, 128), BF16)], [coefficients], name="table")[0]
    node_scratch = [scratch(64, 128) for _ in range(3)]
    node_scratch += [scratch(64, 128, dtype=I32), scratch(64, 128)]
    cells = ((19, 64, 128), F32)
    row_faces = ((24, 128), F32)
    slots = ((64, 128), F32)
    operand = scratch(192, 384, dtype=BF16)

    def contact(states, stride, first, state, hydro):
        kernel = functools.partial(contact_kernel, 0, first, stride)
        return call(
            kernel,
            [slots, slots],
            [recv_partner, recv, states, state, recv_row, hydro, table],
            [scratch(1024, 128) for _ in range(6)] + [scratch(4, 64, 128)],
            scalars=1,
            name="contact",
        )

    def loads(payload, local, state):
        back = exchange(payload, across, 32)
        partial = call(
            loads_kernel,
            [slots],
            [back, local, state, body_nodes, send, recv_row, route2, route_col],
            name="loads",
        )[0]
        return exchange(partial, ("gy",), 8)

    def halo(post, y_up, y_down):
        y_low, y_high = neighbours(y_up, y_down, "gy")
        x_up, x_down = call(
            faces_x_kernel, [((80, 128), F32)] * 2, [post, y_low, y_high], name="faces_x"
        )
        x_low, x_high = neighbours(x_up, x_down, "gx")
        z_up, z_down = call(
            faces_z_kernel,
            [((16, 128), F32)] * 2,
            [post, y_low, y_high, x_low, x_high],
            name="faces_z",
        )
        z_low, z_high = neighbours(z_up, z_down, "gz")
        return [y_low, y_high, x_low, x_high, z_low, z_high]

    post, y_up, y_down, hydro = call(
        first_fluid_kernel,
        [cells, row_faces, row_faces, slots],
        [recv, populations, solid],
        [operand, scratch(384, 256), scratch(3, 64, 128), scratch(3, 64, 128)] + node_scratch,
        name="fluid_one",
    )
    payload, local = contact(recv, 24, 22, state, hydro)
    totals = loads(payload, local, state)
    halos = halo(post, y_up, y_down)
    fluid, hydro, interp = call(
        stream_interp_kernel,
        [((19, 4, 16, 128), F32), slots, ((3, 64, 128), F32)],
        [post, solid, recv] + halos,
        [operand] + node_scratch,
        name="stream_interp",
    )
    packed, state = call(
        middle_kernel,
        [((128, 128), F32), ((24, 64), F32)],
        [totals, state, send, route2, route_col],
        [scratch(128, 128)],
        name="middle",
    )
    states = exchange(packed, across, 32)
    post, y_up, y_down = call(
        second_fluid_kernel,
        [cells, row_faces, row_faces],
        [recv, states, fluid, solid, interp],
        [scratch(384, 256), scratch(3, 64, 128)] + node_scratch,
        name="fluid_two",
    )
    payload, local = contact(states, 4, 0, state, hydro)
    totals = loads(payload, local, state)
    halos = halo(post, y_up, y_down)
    fluid = call(
        stream_kernel, [((19, 4, 16, 128), F32)], [post, solid] + halos, name="stream"
    )[0]
    centre, motion = call(
        last_kernel, [((3, 64), F32), ((6, 64), F32)], [totals, state], name="last"
    )
    return fluid, centre, motion


def solution(mesh):
    in_specs = (
        P(None, "gx", "gy", "gz"),
        P("gx", "gy", "gz"),
        P(("gx", "gz"), None, None),
        P(None, "gy", ("gx", "gz")),
        P(None, ("gx", "gz")),
        P(None, ("gx", "gz")),
        P(None, ("gx", "gz")),
        P(None, "gy", ("gx", "gz")),
        P("gy", ("gx", "gz")),
        P("gy", ("gx", "gz"), None),
        P(("gx", "gz"), None),
        P(("gx", "gz"), None),
    )
    out_specs = (P(None, "gx", "gy", "gz"), P(None, ("gx", "gz")), P(None, ("gx", "gz")))
    return jax.shard_map(
        per_device, mesh=mesh, in_specs=in_specs, out_specs=out_specs, check_vma=False
    )
```

profile of v0, /device:TPU:1, one launch (start us, length us, event | category | flops | bytes accessed | tf_op | source)
XLA Modules:
  0.0 185.3 jit_solution(3126423830142381130)
XLA Ops:
  3.7 2.7 %pack.1 = (f32[768,128]{1,0:T(8,128)}, f32[24,64]{1,0:T(8,128)}) custom-call(f32[3,64,64]{2,1,0:T(8,128)} %body.5, f32[3,64,64]{2,1,0:T(8,128)} %frac.1, s32[64,64]{1,0:T(8,128)} %cell.1, f32[3,64]{1,0:T(4,128)} %centers.1, f32[3,64]{1,0:T(4,128)} %angles.1, f32[6,64]{1,0:T(8,128)} %velocity.1, f32[1,128]{1,0:T(1,128)} %convert_element_type.13.send, ...), custom_call_target="tpu_custom_call" | custom-call | tf_op jit(solution)/shard_map/pack/pallas_call | solution.py:709
  6.4 8.6 %all-to-all-start = ((f32[32,24,128]{2,1,0:T(8,128)}), f32[32,24,128]{2,1,0:T(8,128)S(1)}, u32[]{:S(2)}, u32[]{:S(2)}) async-start(f32[32,24,128]{2,1,0:T(8,128)} %bitcast.24), calls=%async_computation | async-start | bytes 786432 | tf_op jit(solution)/shard_map/all_to_all | solution.py:725
  16.2 6.7 %table.1 = bf16[64,256,128]{2,1,0:T(8,128)(2,1)} custom-call(f32[64,16,256]{2,1,0:T(8,128)} %coefs.1), custom_call_target="tpu_custom_call" | custom-call | tf_op jit(solution)/shard_map/table/pallas_call | solution.py:709
  22.9 2.3 %all-to-all-done = f32[32,24,128]{2,1,0:T(8,128)S(1)} async-done(((f32[32,24,128]{2,1,0:T(8,128)}), f32[32,24,128]{2,1,0:T(8,128)S(1)}, u32[]{:S(2)}, u32[]{:S(2)}) %all-to-all-start) | async-done | bytes 393248 | tf_op jit(solution)/shard_map/all_to_all | solution.py:725
  25.9 18.0 %fluid_one.1 = (f32[19,64,128]{2,1,0:T(8,128)}, f32[24,128]{1,0:T(8,128)}, f32[24,128]{1,0:T(8,128)}, f32[64,128]{1,0:T(8,128)}) custom-call(f32[768,128]{1,0:T(8,128)} %bitcast.16, f32[19,4,16,128]{3,2,1,0:T(8,128)} %fluid.1, s32[4,16,128]{2,1,0:T(8,128)} %solid.7), custom_call_target="tpu_custom_call" | custom-call | tf_op jit(solution)/shard_map/fluid_one/pallas_call | solution.py:709
  44.0 12.8 %contact.2 = (f32[64,128]{1,0:T(8,128)}, f32[64,128]{1,0:T(8,128)}) custom-call(s32[1,128]{1,0:T(1,128)} %partners.3, f32[768,128]{1,0:T(8,128)} %bitcast.17, f32[768,128]{1,0:T(8,128)} %bitcast.18, f32[24,64]{1,0:T(8,128)} %get-tuple-element.32.state, f32[1,128]{1,0:T(1,128)} %convert_element_type.17.recv_row, f32[64,128]{1,0:T(8,128)} %get-tuple-element.33.hydro, ...), custom_call_target="tpu_custom_call" | custom-call | tf_op jit(solution)/shard_map/contact/pallas_call | solution.py:709
  56.8 12.5 %all_to_all.30 = f32[32,2,128]{2,1,0:T(2,128)} all-to-all(f32[32,2,128]{2,1,0:T(2,128)} %bitcast.33), channel_id=1, replica_groups=mesh['gx'=4,'gy'=8,'gz'=8] {'gx','gz'}, dimensions={0} | all-to-all | bytes 65536 | tf_op jit(solution)/shard_map/all_to_all | solution.py:725
  69.3 2.0 %loads.2 = f32[64,128]{1,0:T(8,128)} custom-call(f32[64,128]{1,0:T(8,128)} %bitcast.29, f32[64,128]{1,0:T(8,128)} %get-tuple-element.35.local, f32[24,64]{1,0:T(8,128)} %get-tuple-element.32.state, f32[3,64,64]{2,1,0:T(8,128)} %body.5, f32[1,128]{1,0:T(1,128)} %convert_element_type.13.send, f32[1,128]{1,0:T(1,128)} %convert_element_type.17.recv_row, ...), custom_call_target="tpu_custom_call" | custom-call | tf_op jit(solution)/shard_map/loads/pallas_call | solution.py:709
  71.3 15.3 %all_to_all.31 = f32[8,8,128]{2,1,0:T(8,128)} all-to-all(f32[8,8,128]{2,1,0:T(8,128)} %bitcast.30), channel_id=1, replica_groups=mesh['gx'=4,'gy'=8,'gz'=8] {'gy'}, dimensions={0} | all-to-all | bytes 65536 | tf_op jit(solution)/shard_map/all_to_all | solution.py:725
  88.3 5.2 %all-to-all-start.3 = ((f32[32,4,128]{2,1,0:T(4,128)}), f32[32,4,128]{2,1,0:T(4,128)S(1)}, u32[]{:S(2)}, u32[]{:S(2)}) async-start(f32[32,4,128]{2,1,0:T(4,128)} %bitcast.31), calls=%async_computation.3 | async-start | bytes 131072 | tf_op jit(solution)/shard_map/all_to_all | solution.py:725
  93.9 2.4 %collective-permute-start.1 = (f32[24,128]{1,0:T(8,128)S(1)}, f32[24,128]{1,0:T(8,128)S(1)}, u32[]{:S(2)}, u32[]{:S(2)}) collective-permute-start(f32[24,128]{1,0:T(8,128)S(1)} %copy-done.16), channel_id=1, source_target_pairs={{8,0},{16,8},{24,16},{32,24},{40,32},{48,40},{56,48},{0,56},{9,1},... | collective-permute-start | bytes 36872 | tf_op jit(solution)/shard_map/ppermute | solution.py:735
  107.5 3.6 %collective-permute-start.4 = (f32[16,128]{1,0:T(8,128)}, f32[16,128]{1,0:T(8,128)S(1)}, u32[]{:S(2)}, u32[]{:S(2)}) collective-permute-start(f32[16,128]{1,0:T(8,128)} %get-tuple-element.42), channel_id=1, source_target_pairs={{0,1},{1,2},{2,3},{3,4},{4,5},{5,6},{6,7},{7,0},{8,9},{9,10},{10,1... | collective-permute-start | bytes 24584 | tf_op jit(solution)/shard_map/ppermute | solution.py:735
  112.1 2.3 %collective-permute-done.5.refs_5_ = f32[16,128]{1,0:T(8,128)S(1)} collective-permute-done((f32[16,128]{1,0:T(8,128)}, f32[16,128]{1,0:T(8,128)S(1)}, u32[]{:S(2)}, u32[]{:S(2)}) %collective-permute-start.5) | collective-permute-done | bytes 8224 | tf_op jit(solution)/shard_map/ppermute | solution.py:735
  115.0 9.8 %stream_interp.1 = (f32[19,4,16,128]{3,2,1,0:T(8,128)}, f32[64,128]{1,0:T(8,128)}, f32[3,64,128]{2,1,0:T(8,128)}) custom-call(f32[19,64,128]{2,1,0:T(8,128)} %get-tuple-element.37.post, s32[4,16,128]{2,1,0:T(8,128)} %solid.7, f32[768,128]{1,0:T(8,128)} %bitcast.19, f32[24,128]{1,0:T(8,128)} %copy-done.10, f32[24,128]{1,0:T(8,128)} %copy-done.11, ...), custom_call_target="tpu_custom_call" | custom-call | tf_op jit(solution)/shard_map/stream_interp/pallas_call | solution.py:709
  125.4 12.7 %contact.3 = (f32[64,128]{1,0:T(8,128)}, f32[64,128]{1,0:T(8,128)}) custom-call(s32[1,128]{1,0:T(1,128)} %partners.3, f32[768,128]{1,0:T(8,128)} %bitcast.20, f32[128,128]{1,0:T(8,128)} %bitcast.22, f32[24,64]{1,0:T(8,128)} %get-tuple-element.53.state, f32[1,128]{1,0:T(1,128)} %convert_element_type.17.recv_row, f32[64,128]{1,0:T(8,128)} %get-tuple-element.54.hydro, ...), custom_call_target="tpu_custom_call" | custom-call | tf_op jit(solution)/shard_map/contact/pallas_call | solution.py:709
  138.1 6.4 %all-to-all-start.4 = ((f32[32,2,128]{2,1,0:T(2,128)}), f32[32,2,128]{2,1,0:T(2,128)S(1)}, u32[]{:S(2)}, u32[]{:S(2)}) async-start(f32[32,2,128]{2,1,0:T(2,128)} %bitcast.32), calls=%async_computation.4 | async-start | bytes 65536 | tf_op jit(solution)/shard_map/all_to_all | solution.py:725
  144.6 10.9 %fluid_two.1 = (f32[19,64,128]{2,1,0:T(8,128)}, f32[24,128]{1,0:T(8,128)}, f32[24,128]{1,0:T(8,128)}) custom-call(f32[768,128]{1,0:T(8,128)} %bitcast.21, f32[128,128]{1,0:T(8,128)} %bitcast.23, f32[19,4,16,128]{3,2,1,0:T(8,128)} %get-tuple-element.44.fluid, s32[4,16,128]{2,1,0:T(8,128)} %solid.7, f32[3,64,128]{2,1,0:T(8,128)} %get-tuple-element.45.interp), custom_call_target="tpu_custom_call" | custom-call | tf_op jit(solution)/shard_map/fluid_two/pallas_call | solution.py:709
  155.4 3.0 %collective-permute-start.7 = (f32[24,128]{1,0:T(8,128)}, f32[24,128]{1,0:T(8,128)S(1)}, u32[]{:S(2)}, u32[]{:S(2)}) collective-permute-start(f32[24,128]{1,0:T(8,128)} %get-tuple-element.48), channel_id=1, source_target_pairs={{8,0},{16,8},{24,16},{32,24},{40,32},{48,40},{56,48},{0,56},{9,1},... | collective-permute-start | bytes 36872 | tf_op jit(solution)/shard_map/ppermute | solution.py:735
  159.0 2.0 %loads.3 = f32[64,128]{1,0:T(8,128)} custom-call(f32[64,128]{1,0:T(8,128)} %bitcast.28, f32[64,128]{1,0:T(8,128)} %get-tuple-element.56.local, f32[24,64]{1,0:T(8,128)} %get-tuple-element.53.state, f32[3,64,64]{2,1,0:T(8,128)} %body.5, f32[1,128]{1,0:T(1,128)} %convert_element_type.13.send, f32[1,128]{1,0:T(1,128)} %convert_element_type.17.recv_row, ...), custom_call_target="tpu_custom_call" | custom-call | tf_op jit(solution)/shard_map/loads/pallas_call | solution.py:709
  161.0 3.3 %all-to-all-start.5 = ((f32[8,8,128]{2,1,0:T(8,128)}), f32[8,8,128]{2,1,0:T(8,128)S(1)}, u32[]{:S(2)}, u32[]{:S(2)}) async-start(f32[8,8,128]{2,1,0:T(8,128)} %bitcast.27), calls=%async_computation.5 | async-start | bytes 65536 | tf_op jit(solution)/shard_map/all_to_all | solution.py:725
  172.5 1.9 %faces_z.3 = (f32[16,128]{1,0:T(8,128)}, f32[16,128]{1,0:T(8,128)}) custom-call(f32[19,64,128]{2,1,0:T(8,128)} %get-tuple-element.46.post, f32[24,128]{1,0:T(8,128)} %copy-done.8, f32[24,128]{1,0:T(8,128)} %copy-done.9, f32[80,128]{1,0:T(8,128)} %copy-done.3, f32[80,128]{1,0:T(8,128)} %copy-done.5), custom_call_target="tpu_custom_call" | custom-call | tf_op jit(solution)/shard_map/faces_z/pallas_call | solution.py:709
  174.4 2.8 %collective-permute-start.10 = (f32[16,128]{1,0:T(8,128)}, f32[16,128]{1,0:T(8,128)S(1)}, u32[]{:S(2)}, u32[]{:S(2)}) collective-permute-start(f32[16,128]{1,0:T(8,128)} %get-tuple-element.51), channel_id=1, source_target_pairs={{0,1},{1,2},{2,3},{3,4},{4,5},{5,6},{6,7},{7,0},{8,9},{9,10},{10,1... | collective-permute-start | bytes 24584 | tf_op jit(solution)/shard_map/ppermute | solution.py:735
  178.2 2.3 %collective-permute-done.11.refs_5_ = f32[16,128]{1,0:T(8,128)S(1)} collective-permute-done((f32[16,128]{1,0:T(8,128)}, f32[16,128]{1,0:T(8,128)S(1)}, u32[]{:S(2)}, u32[]{:S(2)}) %collective-permute-start.11) | collective-permute-done | bytes 8224 | tf_op jit(solution)/shard_map/ppermute | solution.py:735
  181.1 2.3 %stream.1 = f32[19,4,16,128]{3,2,1,0:T(8,128)} custom-call(f32[19,64,128]{2,1,0:T(8,128)} %get-tuple-element.46.post, s32[4,16,128]{2,1,0:T(8,128)} %solid.7, f32[24,128]{1,0:T(8,128)} %copy-done.8, f32[24,128]{1,0:T(8,128)} %copy-done.9, f32[80,128]{1,0:T(8,128)} %copy-done.3, f32[80,128]{1,0:T(8,128)} %copy-done.5, f32[16,128]{1,0:T(8,128)} %copy-done.13, ...), custom_call_target="tpu_custom_call" | custom-call | tf_op jit(solution)/shard_map/stream/pallas_call | solution.py:709
  (67 shorter events, 32.9 us)
Async XLA Ops:
  6.4 18.7 %all-to-all-start = ((f32[32,24,128]{2,1,0:T(8,128)}), f32[32,24,128]{2,1,0:T(8,128)S(1)}, u32[]{:S(2)}, u32[]{:S(2)}) async-start(f32[32,24,128]{2,1,0:T(8,128)} %bitcast.24), calls=%async_computation | async-start | bytes 786432 | tf_op jit(solution)/shard_map/all_to_all | solution.py:725
  25.2 0.8 copy-start
  44.0 49.6 %copy-start.17 = (f32[24,128]{1,0:T(8,128)S(1)}, f32[24,128]{1,0:T(8,128)}, u32[]{:S(2)}) copy-start(f32[24,128]{1,0:T(8,128)} %get-tuple-element.38) | copy-start | bytes 36868
  44.0 49.9 %copy-start.16 = (f32[24,128]{1,0:T(8,128)S(1)}, f32[24,128]{1,0:T(8,128)}, u32[]{:S(2)}) copy-start(f32[24,128]{1,0:T(8,128)} %get-tuple-element.39) | copy-start | bytes 36868
  88.3 36.5 %all-to-all-start.3 = ((f32[32,4,128]{2,1,0:T(4,128)}), f32[32,4,128]{2,1,0:T(4,128)S(1)}, u32[]{:S(2)}, u32[]{:S(2)}) async-start(f32[32,4,128]{2,1,0:T(4,128)} %bitcast.31), calls=%async_computation.3 | async-start | bytes 131072 | tf_op jit(solution)/shard_map/all_to_all | solution.py:725
  93.6 4.1 %collective-permute-start = (f32[24,128]{1,0:T(8,128)S(1)}, f32[24,128]{1,0:T(8,128)S(1)}, u32[]{:S(2)}, u32[]{:S(2)}) collective-permute-start(f32[24,128]{1,0:T(8,128)S(1)} %copy-done.17), channel_id=1, source_target_pairs={{0,8},{8,16},{16,24},{24,32},{32,40},{40,48},{48,56},{56,0},{1,9},... | collective-permute-start | bytes 36872 | tf_op jit(solution)/shard_map/ppermute | solution.py:735
  93.9 3.8 %collective-permute-start.1 = (f32[24,128]{1,0:T(8,128)S(1)}, f32[24,128]{1,0:T(8,128)S(1)}, u32[]{:S(2)}, u32[]{:S(2)}) collective-permute-start(f32[24,128]{1,0:T(8,128)S(1)} %copy-done.16), channel_id=1, source_target_pairs={{8,0},{16,8},{24,16},{32,24},{40,32},{48,40},{56,48},{0,56},{9,1},... | collective-permute-start | bytes 36872 | tf_op jit(solution)/shard_map/ppermute | solution.py:735
  100.0 4.3 %collective-permute-start.2 = (f32[80,128]{1,0:T(8,128)}, f32[80,128]{1,0:T(8,128)S(1)}, u32[]{:S(2)}, u32[]{:S(2)}) collective-permute-start(f32[80,128]{1,0:T(8,128)} %get-tuple-element.40), channel_id=1, source_target_pairs={{0,64},{64,128},{128,192},{192,0},{1,65},{65,129},{129,193},{193,1... | collective-permute-start | bytes 122888 | tf_op jit(solution)/shard_map/ppermute | solution.py:735
  101.5 3.1 %collective-permute-start.3 = (f32[80,128]{1,0:T(8,128)}, f32[80,128]{1,0:T(8,128)S(1)}, u32[]{:S(2)}, u32[]{:S(2)}) collective-permute-start(f32[80,128]{1,0:T(8,128)} %get-tuple-element.41), channel_id=1, source_target_pairs={{64,0},{128,64},{192,128},{0,192},{65,1},{129,65},{193,129},{1,193... | collective-permute-start | bytes 122888 | tf_op jit(solution)/shard_map/ppermute | solution.py:735
  104.4 0.6 copy-start.2
  107.5 4.6 %collective-permute-start.4 = (f32[16,128]{1,0:T(8,128)}, f32[16,128]{1,0:T(8,128)S(1)}, u32[]{:S(2)}, u32[]{:S(2)}) collective-permute-start(f32[16,128]{1,0:T(8,128)} %get-tuple-element.42), channel_id=1, source_target_pairs={{0,1},{1,2},{2,3},{3,4},{4,5},{5,6},{6,7},{7,0},{8,9},{9,10},{10,1... | collective-permute-start | bytes 24584 | tf_op jit(solution)/shard_map/ppermute | solution.py:735
  111.1 3.3 %collective-permute-start.5 = (f32[16,128]{1,0:T(8,128)}, f32[16,128]{1,0:T(8,128)S(1)}, u32[]{:S(2)}, u32[]{:S(2)}) collective-permute-start(f32[16,128]{1,0:T(8,128)} %get-tuple-element.43), channel_id=1, source_target_pairs={{1,0},{2,1},{3,2},{4,3},{5,4},{6,5},{7,6},{0,7},{9,8},{10,9},{11,1... | collective-permute-start | bytes 24584 | tf_op jit(solution)/shard_map/ppermute | solution.py:735
  112.1 2.3 %copy-start.12 = (f32[16,128]{1,0:T(8,128)}, f32[16,128]{1,0:T(8,128)S(1)}, u32[]{:S(2)}) copy-start(f32[16,128]{1,0:T(8,128)S(1)} %collective-permute-done.4.refs_4_) | copy-start | bytes 24580
  124.8 0.6 copy-start.1
  138.1 20.3 %all-to-all-start.4 = ((f32[32,2,128]{2,1,0:T(2,128)}), f32[32,2,128]{2,1,0:T(2,128)S(1)}, u32[]{:S(2)}, u32[]{:S(2)}) async-start(f32[32,2,128]{2,1,0:T(2,128)} %bitcast.32), calls=%async_computation.4 | async-start | bytes 65536 | tf_op jit(solution)/shard_map/all_to_all | solution.py:725
  155.4 8.9 %collective-permute-start.6 = (f32[24,128]{1,0:T(8,128)}, f32[24,128]{1,0:T(8,128)S(1)}, u32[]{:S(2)}, u32[]{:S(2)}) collective-permute-start(f32[24,128]{1,0:T(8,128)} %get-tuple-element.47), channel_id=1, source_target_pairs={{0,8},{8,16},{16,24},{24,32},{32,40},{40,48},{48,56},{56,0},{1,9},... | collective-permute-start | bytes 36872 | tf_op jit(solution)/shard_map/ppermute | solution.py:735
  155.4 8.9 %collective-permute-start.7 = (f32[24,128]{1,0:T(8,128)}, f32[24,128]{1,0:T(8,128)S(1)}, u32[]{:S(2)}, u32[]{:S(2)}) collective-permute-start(f32[24,128]{1,0:T(8,128)} %get-tuple-element.48), channel_id=1, source_target_pairs={{8,0},{16,8},{24,16},{32,24},{40,32},{48,40},{56,48},{0,56},{9,1},... | collective-permute-start | bytes 36872 | tf_op jit(solution)/shard_map/ppermute | solution.py:735
  158.4 0.6 copy-start.7
  161.0 22.3 %all-to-all-start.5 = ((f32[8,8,128]{2,1,0:T(8,128)}), f32[8,8,128]{2,1,0:T(8,128)S(1)}, u32[]{:S(2)}, u32[]{:S(2)}) async-start(f32[8,8,128]{2,1,0:T(8,128)} %bitcast.27), calls=%async_computation.5 | async-start | bytes 65536 | tf_op jit(solution)/shard_map/all_to_all | solution.py:725
  166.7 4.6 %collective-permute-start.8 = (f32[80,128]{1,0:T(8,128)}, f32[80,128]{1,0:T(8,128)S(1)}, u32[]{:S(2)}, u32[]{:S(2)}) collective-permute-start(f32[80,128]{1,0:T(8,128)} %get-tuple-element.49), channel_id=1, source_target_pairs={{0,64},{64,128},{128,192},{192,0},{1,65},{65,129},{129,193},{193,1... | collective-permute-start | bytes 122888 | tf_op jit(solution)/shard_map/ppermute | solution.py:735
  168.1 3.4 %collective-permute-start.9 = (f32[80,128]{1,0:T(8,128)}, f32[80,128]{1,0:T(8,128)S(1)}, u32[]{:S(2)}, u32[]{:S(2)}) collective-permute-start(f32[80,128]{1,0:T(8,128)} %get-tuple-element.50), channel_id=1, source_target_pairs={{64,0},{128,64},{192,128},{0,192},{65,1},{129,65},{193,129},{1,193... | collective-permute-start | bytes 122888 | tf_op jit(solution)/shard_map/ppermute | solution.py:735
  174.4 3.8 %collective-permute-start.10 = (f32[16,128]{1,0:T(8,128)}, f32[16,128]{1,0:T(8,128)S(1)}, u32[]{:S(2)}, u32[]{:S(2)}) collective-permute-start(f32[16,128]{1,0:T(8,128)} %get-tuple-element.51), channel_id=1, source_target_pairs={{0,1},{1,2},{2,3},{3,4},{4,5},{5,6},{6,7},{7,0},{8,9},{9,10},{10,1... | collective-permute-start | bytes 24584 | tf_op jit(solution)/shard_map/ppermute | solution.py:735
  177.2 3.3 %collective-permute-start.11 = (f32[16,128]{1,0:T(8,128)}, f32[16,128]{1,0:T(8,128)S(1)}, u32[]{:S(2)}, u32[]{:S(2)}) collective-permute-start(f32[16,128]{1,0:T(8,128)} %get-tuple-element.52), channel_id=1, source_target_pairs={{1,0},{2,1},{3,2},{4,3},{5,4},{6,5},{7,6},{0,7},{9,8},{10,9},{11,1... | collective-permute-start | bytes 24584 | tf_op jit(solution)/shard_map/ppermute | solution.py:735
  178.2 2.3 %copy-start.13 = (f32[16,128]{1,0:T(8,128)}, f32[16,128]{1,0:T(8,128)S(1)}, u32[]{:S(2)}) copy-start(f32[16,128]{1,0:T(8,128)S(1)} %collective-permute-done.10.refs_4_) | copy-start | bytes 24580
  (10 other events, 6.0 us)
where the time goes:
time: 186 us; the launch traced here: 185 us
  Pallas kernels  90.4 us (49%)
  starting transfers between devices  41 us (22%)
  blocking collectives  27.7 us (15%)
  waiting for transfers between devices  14 us (8%)
  local copies, waits for them, and re-layouts  7.86 us (4%)
  other arithmetic  3.6 us (2%)
    pallas_call x16, Pallas kernels, call(): pl.pallas_call(kernel, out_shape=shapes, in_specs=[SMEM] * scalars + [VME...  90.4 us
    all_to_all x2, blocking collectives, exchange(): lax.all_to_all(value.reshape(parts, rows // parts, lanes), axes, split_ax...  27.7 us
    all_to_all x4, starting transfers between devices, exchange(): lax.all_to_all(value.reshape(parts, rows // parts, lanes), axes, split_ax...  23.6 us
    ppermute x12, starting transfers between devices, neighbours(): return (lax.ppermute(up, axis, forward), lax.ppermute(down, axis, backward))  17.5 us
    ppermute x12, waiting for transfers between devices, neighbours(): return (lax.ppermute(up, axis, forward), lax.ppermute(down, axis, backward))  11.7 us
    unnamed x36, local copies, waits for them, and re-layouts  7.16 us
  transfers between devices with their start and end apart: 16, of which 10 were waited for; matrix products, arithmetic and copies ran while one was open for 1% of the time, Pallas kernels for 21%

commit v1 on v0

--- a/solution.py
+++ b/solution.py
@@ -35,6 +35,8 @@
 WEIGHTS = WEIGHTS + [float(np.float32(1.0 / 36.0))] * 12
 OPPOSITE = [0, 2, 1, 4, 3, 6, 5, 8, 7, 10, 9, 12, 11, 14, 13, 16, 15, 18, 17]
 TAU = 0.9
+CONTACT_STEP = 8
+PAIR_STEP = 4
 STIFF = 0.5
 CONTACT = 0.05
 DT = 0.05
@@ -240,16 +242,17 @@
     rel = [arm[i] + (field(pst, 9 + i) - held(9 + i)) for i in range(3)]
     rot = [[held(3 * i + j) for j in range(3)] for i in range(3)]
     for axis, (kinds, slopes) in enumerate(((xt, xs), (yt, ys), (zt, zs))):
+        rows = (lambda n: pl.ds(n * 64, 64)) if axis == 1 else (lambda n: pl.ds(n, 64, stride=24))
         y = rot[0][axis] * rel[0] + rot[1][axis] * rel[1] + rot[2][axis] * rel[2]
         y = jnp.clip(y, -1.0, 1.0)
         twice = 2.0 * y
         t_old, t_new = jnp.ones((64, 128), F32), y
         u_old, u_new = jnp.zeros((64, 128), F32), jnp.ones((64, 128), F32)
-        kinds[pl.ds(0, 64, stride=16), :] = t_old
-        slopes[pl.ds(0, 64, stride=16), :] = u_old
+        kinds[rows(0), :] = t_old
+        slopes[rows(0), :] = u_old
         for n in range(1, 16):
-            kinds[pl.ds(n, 64, stride=16), :] = t_new
-            slopes[pl.ds(n, 64, stride=16), :] = float(n) * u_new
+            kinds[rows(n), :] = t_new
+            slopes[rows(n), :] = float(n) * u_new
             t_old, t_new = t_new, twice * t_new - t_old
             u_old, u_new = u_new, twice * u_new - u_old
     low = iota((16, 128), 1) < 64
@@ -260,7 +263,7 @@
         grain_a = jnp.maximum(partners[0, slot], 0)
         grain_b = jnp.maximum(partners[0, slot + 1], 0)
         left = jnp.concatenate([table[grain_a], table[grain_b]], axis=1)
-        at = pl.ds(pl.multiple_of(p * 16, 16), 16)
+        at = pl.ds(pl.multiple_of(p * 24, 8), 16)
         z_value, z_slope = zt[at, :], zs[at, :]
         blocks = []
         for keep in (low, jnp.logical_not(low)):
@@ -270,28 +273,28 @@
             blocks += [both[0], both[1], both[2], both[0], both[1], both[0], zero, zero]
         right = jnp.concatenate(blocks, axis=0)
         sums = dot(left, right)
-        y_kind, y_slope = yt[at, :], ys[at, :]
         value = jnp.zeros((16, 128), F32)
         value_y = jnp.zeros((16, 128), F32)
         value_z = jnp.zeros((16, 128), F32)
         for b in range(16):
             plain = sums[b * 16 : (b + 1) * 16, :128]
             steep = sums[b * 16 : (b + 1) * 16, 128:]
-            value = value + plain * y_kind[b : b + 1]
-            value_y = value_y + plain * y_slope[b : b + 1]
-            value_z = value_z + steep * y_kind[b : b + 1]
+            y_kind, y_slope = yt[pl.ds(b * 64 + p, 1), :], ys[pl.ds(b * 64 + p, 1), :]
+            value = value + plain * y_kind
+            value_y = value_y + plain * y_slope
+            value_z = value_z + steep * y_kind
         x_kind, x_slope = xt[at, :], xs[at, :]
         for i, term in enumerate(
             (value * x_kind, value * x_slope, value_y * x_kind, value_z * x_kind)
         ):
             found[i, pl.ds(p, 1), :] = jnp.sum(term, axis=0, keepdims=True)
 
-    def two(i, carry):
-        one(2 * i)
-        one(2 * i + 1)
+    def several(i, carry):
+        for k in range(CONTACT_STEP):
+            one(CONTACT_STEP * i + k)
         return carry
 
-    lax.fori_loop(0, 32, two, 0)
+    lax.fori_loop(0, 64 // CONTACT_STEP, several, 0)
     level = found[0]
     grad = [found[1], found[2], found[3]]
     alive = jnp.sum(hold_hot.reshape(64, 128) * jnp.where(half, 1.0, 0.0), axis=1, keepdims=True)
@@ -321,23 +324,39 @@
     alive[...] = jnp.where(named > 0.5, 1.0, 0.0)
 
 
+def wide(row):
+    return jnp.broadcast_to(row, (16, 128)).astype(BF16)
+
+
 def node_weights(refs, p):
     fx, fy, fz, base, _ = refs
     at = pl.ds(p, 1)
     cell = base[at, :]
     x, y, z = cell >> 11, (cell >> 7) & 15, cell & 127
-    gap = iota((128, 128), 0) - z
     up = fz[at, :]
-    along_z = jnp.where(gap == 0, 1.0 - up, jnp.where(gap == 1, up, 0.0))
-    gap = iota((16, 128), 0) - y
+    ends = []
+    for weight in (1.0 - up, up):
+        high = weight.astype(BF16).astype(F32)
+        ends.append((wide(high), wide(weight - high)))
+    z_low, z_high = wide(z.astype(F32)), wide((z + 1).astype(F32))
+    zero = jnp.zeros((16, 128), BF16)
+    pieces = ([], [])
+    for block in range(8):
+        row = (iota((16, 128), 0) + block * 16).astype(F32).astype(BF16)
+        at_low, at_high = row == z_low, row == z_high
+        for i in range(2):
+            upper = jnp.where(at_high, ends[1][i], zero)
+            pieces[i].append(jnp.where(at_low, ends[0][i], upper))
+    row = iota((16, 128), 0)
     up = fy[at, :]
-    along_y = jnp.where(gap == 0, 1.0 - up, jnp.where(gap == 1, up, 0.0))
+    along_y = jnp.where(row == y, 1.0 - up, jnp.where(row == y + 1, up, 0.0))
     up = fx[at, :]
     both = []
     for cx in range(4):
         weight = jnp.where(x == cx, 1.0 - up, jnp.where(x == cx - 1, up, 0.0))
         both.append(weight * along_y)
-    return split2(along_z), jnp.concatenate(both, axis=0)
+    along_z = [jnp.concatenate(piece, axis=0) for piece in pieces]
+    return along_z, jnp.concatenate(both, axis=0)
 
 
 def pair_weights(refs, i):
@@ -374,19 +393,47 @@
         operand[rows, 256:384] = low
 
 
-def interpolate(operand, high, low, across):
-    along = dot(operand[...], jnp.concatenate([high, low, high], axis=0))
-    return [
-        jnp.sum(along[c * 64 : (c + 1) * 64] * across, axis=0, keepdims=True) for c in range(3)
-    ]
-
-
-def spread_pair(total, force, high, low, across):
-    push = jnp.concatenate([force[c] * across for c in range(3)], axis=0)
-    push_high, push_low = split2(push)
-    total[...] += dot_nt(
-        jnp.concatenate([push_high, push_low], axis=0), jnp.concatenate([high, low], axis=0)
-    )
+def interp_loop(refs, operand, interp, kept=None):
+    def several(i, carry):
+        for step in range(PAIR_STEP):
+            at = PAIR_STEP * i + step
+            high, low, across = pair_weights(refs, at)
+            if kept is not None:
+                kept[0][at, 0:128, :] = high
+                kept[0][at, 128:256, :] = low
+                kept[1][at] = across
+            along = dot(operand[...], jnp.concatenate([high, low, high], axis=0))
+            for c in range(3):
+                found = jnp.sum(along[c * 64 : (c + 1) * 64] * across, axis=0, keepdims=True)
+                for k in range(2):
+                    interp[c, pl.ds(2 * at + k, 1), :] = found[:, k * 128 : (k + 1) * 128]
+        return carry
+
+    lax.fori_loop(0, 32 // PAIR_STEP, several, 0)
+
+
+def spread_loop(refs, forces, total, kept=None):
+    total[...] = jnp.zeros((384, 256), F32)
+
+    def several(i, carry):
+        pushes, weights = [], []
+        for step in range(PAIR_STEP):
+            at = PAIR_STEP * i + step
+            if kept is None:
+                high, low, across = pair_weights(refs, at)
+                weights.append(jnp.concatenate([high, low], axis=0))
+            else:
+                weights.append(kept[0][at])
+                across = kept[1][at]
+            push = []
+            for c in range(3):
+                force = [forces[c, pl.ds(2 * at + k, 1), :] for k in range(2)]
+                push.append(jnp.concatenate(force, axis=1) * across)
+            pushes.append(jnp.concatenate(split2(jnp.concatenate(push, axis=0)), axis=0))
+        total[...] += dot_nt(jnp.concatenate(pushes, axis=1), jnp.concatenate(weights, axis=1))
+        return carry
+
+    lax.fori_loop(0, 32 // PAIR_STEP, several, 0)
 
 
 def node_speed(recv, state):
@@ -439,34 +486,17 @@
 
 
 def first_fluid_kernel(
-    recv, fluid, solid, post, y_up, y_down, hydro, operand, total, interp, speeds, *refs
+    recv, fluid, solid, post, y_up, y_down, hydro, operand, total, interp, forces, near, far, *refs
 ):
     get = lambda q: fluid[q].reshape(64, 128)
     density, flow = moments(get)
     flow_operand(flow, operand)
     node_setup(recv, refs)
+    interp_loop(refs, operand, interp, (near, far))
     speed = node_speed(recv, strided(recv, 32, 24, 14))
     for c in range(3):
-        speeds[c] = speed[c]
-    total[...] = jnp.zeros((384, 256), F32)
-    alive = refs[4]
-
-    def pair(i, carry):
-        high, low, across = pair_weights(refs, i)
-        found = interpolate(operand, high, low, across)
-        force = []
-        for c in range(3):
-            sides = []
-            for k in range(2):
-                at = pl.ds(2 * i + k, 1)
-                side = found[c][:, k * 128 : (k + 1) * 128]
-                interp[c, at, :] = side
-                sides.append(STIFF * (speeds[c, at, :] - side) * alive[at, :])
-            force.append(jnp.concatenate(sides, axis=1))
-        spread_pair(total, force, high, low, across)
-        return carry
-
-    lax.fori_loop(0, 32, pair, 0)
+        forces[c] = STIFF * (speed[c] - interp[c]) * refs[4][...]
+    spread_loop(refs, forces, total, (near, far))
     hydro[...] = hydro_sums(recv, interp)
     collide(get, density, flow, total, solid, post, y_up, y_down)
 
@@ -558,17 +588,7 @@
     _, flow = moments(lambda q: fluid[q].reshape(64, 128))
     flow_operand(flow, operand)
     node_setup(recv, scratch)
-
-    def pair(i, carry):
-        high, low, across = pair_weights(scratch, i)
-        found = interpolate(operand, high, low, across)
-        for c in range(3):
-            for k in range(2):
-                at = pl.ds(2 * i + k, 1)
-                interp[c, at, :] = found[c][:, k * 128 : (k + 1) * 128]
-        return carry
-
-    lax.fori_loop(0, 32, pair, 0)
+    interp_loop(scratch, operand, interp)
     hydro[...] = hydro_sums(recv, interp)
 
 
@@ -582,18 +602,7 @@
     speed = node_speed(recv, strided(states, 32, 4, 2))
     for c in range(3):
         speeds[c] = STIFF * (speed[c] - interp[c]) * alive[...]
-    total[...] = jnp.zeros((384, 256), F32)
-
-    def pair(i, carry):
-        high, low, across = pair_weights(refs, i)
-        force = [
-            jnp.concatenate([speeds[c, pl.ds(2 * i + k, 1), :] for k in range(2)], axis=1)
-            for c in range(3)
-        ]
-        spread_pair(total, force, high, low, across)
-        return carry
-
-    lax.fori_loop(0, 32, pair, 0)
+    spread_loop(refs, speeds, total)
     collide(get, density, flow, total, solid, post, y_up, y_down)
 
 
@@ -700,20 +709,44 @@
         motion[i : i + 1, :] = rows[12 + i]
 
 
+MICROSECONDS = {
+    "pack": 3,
+    "table": 6,
+    "fluid_one": 11,
+    "contact": 9,
+    "loads": 2,
+    "middle": 2,
+    "faces_x": 2,
+    "faces_z": 2,
+    "stream_interp": 7,
+    "fluid_two": 8,
+    "stream": 2,
+    "last": 1,
+}
 VMEM = pl.BlockSpec(memory_space=pltpu.VMEM)
 SMEM = pl.BlockSpec(memory_space=pltpu.SMEM)
 
 
-def call(kernel, outs, args, scratch=(), scalars=0, name=None):
+def call(kernel, outs, args, scratch=(), scalars=0, name=None, after=()):
+    count = len(args)
+
+    def body(*refs):
+        kernel(*refs[:count], *refs[count + len(after) :])
+
     shapes = [jax.ShapeDtypeStruct(shape, dtype) for shape, dtype in outs]
     return pl.pallas_call(
-        kernel,
+        body,
         out_shape=shapes,
-        in_specs=[SMEM] * scalars + [VMEM] * (len(args) - scalars),
+        in_specs=[SMEM] * scalars
+        + [VMEM] * (len(args) - scalars)
+        + [pl.BlockSpec(memory_space=pl.ANY)] * len(after),
         out_specs=[VMEM] * len(outs),
         scratch_shapes=list(scratch),
         name=name,
-    )(*args)
+        cost_estimate=pl.CostEstimate(
+            flops=0, transcendentals=0, bytes_accessed=MICROSECONDS[name] * 3_690_000
+        ),
+    )(*args, *after)
 
 
 def scratch(*shape, dtype=F32):
@@ -777,18 +810,22 @@
             kernel,
             [slots, slots],
             [recv_partner, recv, states, state, recv_row, hydro, table],
-            [scratch(1024, 128) for _ in range(6)] + [scratch(4, 64, 128)],
+            [scratch(1536, 128) for _ in range(2)]
+            + [scratch(1024, 128) for _ in range(2)]
+            + [scratch(1536, 128) for _ in range(2)]
+            + [scratch(4, 64, 128)],
             scalars=1,
             name="contact",
         )
 
-    def loads(payload, local, state):
+    def loads(payload, local, state, after=()):
         back = exchange(payload, across, 32)
         partial = call(
             loads_kernel,
             [slots],
             [back, local, state, body_nodes, send, recv_row, route2, route_col],
             name="loads",
+            after=after,
         )[0]
         return exchange(partial, ("gy",), 8)
 
@@ -811,12 +848,15 @@
         first_fluid_kernel,
         [cells, row_faces, row_faces, slots],
         [recv, populations, solid],
-        [operand, scratch(384, 256), scratch(3, 64, 128), scratch(3, 64, 128)] + node_scratch,
+        [operand, scratch(384, 256), scratch(3, 64, 128), scratch(3, 64, 128)]
+        + [scratch(32, 256, 256, dtype=BF16), scratch(32, 64, 256)]
+        + node_scratch,
         name="fluid_one",
+        after=[table],
     )
     payload, local = contact(recv, 24, 22, state, hydro)
-    totals = loads(payload, local, state)
     halos = halo(post, y_up, y_down)
+    totals = loads(payload, local, state, halos[4:])
     fluid, hydro, interp = call(
         stream_interp_kernel,
         [((19, 4, 16, 128), F32), slots, ((3, 64, 128), F32)],
@@ -830,6 +870,7 @@
         [totals, state, send, route2, route_col],
         [scratch(128, 128)],
         name="middle",
+        after=[interp],
     )
     states = exchange(packed, across, 32)
     post, y_up, y_down = call(

time: 186 us -> 153 us (0.82)
  Pallas kernels: 90.4 us -> 63.8 us
  blocking collectives: 27.7 us -> 15.1 us
  starting transfers between devices: 41 us -> 47.2 us
    pallas_call x16, Pallas kernels: 90.4 us -> 63.8 us  [call(): pl.pallas_call(body, out_shape=shapes, in_specs=[SMEM] * scalars + [VMEM]...]
    all_to_all x2 -> x1, blocking collectives: 27.7 us -> 15.1 us  [exchange(): lax.all_to_all(value.reshape(parts, rows // parts, lanes), axes, split_ax...]
    all_to_all x4 -> x5, starting transfers between devices: 23.6 us -> 28.6 us  [exchange(): lax.all_to_all(value.reshape(parts, rows // parts, lanes), axes, split_ax...]
    all_to_all x4 -> x5, waiting for transfers between devices: 2.28 us -> 7.12 us  [exchange(): lax.all_to_all(value.reshape(parts, rows // parts, lanes), axes, split_ax...]
    ppermute x12, waiting for transfers between devices: 11.7 us -> 7.32 us  [neighbours(): return (lax.ppermute(up, axis, forward), lax.ppermute(down, axis, backward))]
  transfers between devices with their start and end apart: 16 -> 17, of which waited for: 10 -> 9; matrix products, arithmetic and copies ran while one was open for 1% -> 0% of each run, Pallas kernels for 21% -> 24%
where the time goes in v1:
time: 153 us; the launch traced here: 152 us
  Pallas kernels  63.8 us (42%)
  starting transfers between devices  47.2 us (31%)
  blocking collectives  15.1 us (10%)
  waiting for transfers between devices  14.4 us (9%)
  local copies, waits for them, and re-layouts  7.96 us (5%)
  other arithmetic  2.94 us (2%)
    pallas_call x16, Pallas kernels, call(): pl.pallas_call(body, out_shape=shapes, in_specs=[SMEM] * scalars + [VMEM]...  63.8 us
    all_to_all x5, starting transfers between devices, exchange(): lax.all_to_all(value.reshape(parts, rows // parts, lanes), axes, split_ax...  28.6 us
    ppermute x12, starting transfers between devices, neighbours(): return (lax.ppermute(up, axis, forward), lax.ppermute(down, axis, backward))  18.6 us
    all_to_all x1, blocking collectives, exchange(): lax.all_to_all(value.reshape(parts, rows // parts, lanes), axes, split_ax...  15.1 us
    ppermute x12, waiting for transfers between devices, neighbours(): return (lax.ppermute(up, axis, forward), lax.ppermute(down, axis, backward))  7.32 us
    unnamed x36, local copies, waits for them, and re-layouts  7.26 us
    all_to_all x5, waiting for transfers between devices, exchange(): lax.all_to_all(value.reshape(parts, rows // parts, lanes), axes, split_ax...  7.12 us
  transfers between devices with their start and end apart: 17, of which 9 were waited for; matrix products, arithmetic and copies ran while one was open for 0% of the time, Pallas kernels for 24%

profile of v1, /device:TPU:1, one launch (start us, length us, event | category | flops | bytes accessed | tf_op | source)
XLA Modules:
  0.0 152.3 jit_solution(15278938672517405075)
XLA Ops:
  3.7 2.7 %pack.1 = (f32[768,128]{1,0:T(8,128)}, f32[24,64]{1,0:T(8,128)}) custom-call(f32[3,64,64]{2,1,0:T(8,128)} %refs_3_.7, f32[3,64,64]{2,1,0:T(8,128)} %refs_1_.4, s32[64,64]{1,0:T(8,128)} %refs_2_.2, f32[3,64]{1,0:T(4,128)} %refs_3_.4, f32[3,64]{1,0:T(4,128)} %refs_4_.1, f32[6,64]{1,0:T(8,128)} %refs_5_.1, ...), custom_call_target="tpu_custom_call" | custom-call | bytes 11070000 | tf_op jit(solution)/shard_map/pack/pallas_call | solution.py:737
  6.4 8.6 %all-to-all-start = ((f32[32,24,128]{2,1,0:T(8,128)}), f32[32,24,128]{2,1,0:T(8,128)S(1)}, u32[]{:S(2)}, u32[]{:S(2)}) async-start(f32[32,24,128]{2,1,0:T(8,128)} %bitcast.24), calls=%async_computation | async-start | bytes 786432 | tf_op jit(solution)/shard_map/all_to_all | solution.py:758
  15.0 6.7 %table.1.refs_3_.refs_6_ = bf16[64,256,128]{2,1,0:T(8,128)(2,1)} custom-call(f32[64,16,256]{2,1,0:T(8,128)} %refs_0_.5), custom_call_target="tpu_custom_call" | custom-call | bytes 22140000 | tf_op jit(solution)/shard_map/table/pallas_call | solution.py:737
  21.7 3.5 %all-to-all-done = f32[32,24,128]{2,1,0:T(8,128)S(1)} async-done(((f32[32,24,128]{2,1,0:T(8,128)}), f32[32,24,128]{2,1,0:T(8,128)S(1)}, u32[]{:S(2)}, u32[]{:S(2)}) %all-to-all-start) | async-done | bytes 393248 | tf_op jit(solution)/shard_map/all_to_all | solution.py:758
  25.9 9.5 %fluid_one.1 = (f32[19,64,128]{2,1,0:T(8,128)}, f32[24,128]{1,0:T(8,128)}, f32[24,128]{1,0:T(8,128)}, f32[64,128]{1,0:T(8,128)}) custom-call(f32[768,128]{1,0:T(8,128)} %bitcast.16, f32[19,4,16,128]{3,2,1,0:T(8,128)} %refs_1_.5, s32[4,16,128]{2,1,0:T(8,128)} %refs_1_.7, bf16[64,256,128]{2,1,0:T(8,128)(2,1)} %table.1.refs_3_.refs_6_), custom_call_target="tpu_custom_call" | custom-call | bytes 40590000 | tf_op jit(solution)/shard_map/fluid_one/pallas_call | solution.py:737
  37.1 4.0 %collective-permute-start.1 = (f32[24,128]{1,0:T(8,128)}, f32[24,128]{1,0:T(8,128)S(1)}, u32[]{:S(2)}, u32[]{:S(2)}) collective-permute-start(f32[24,128]{1,0:T(8,128)} %get-tuple-element.38), channel_id=1, source_target_pairs={{8,0},{16,8},{24,16},{32,24},{40,32},{48,40},{56,48},{0,56},{9,1},... | collective-permute-start | bytes 36872 | tf_op jit(solution)/shard_map/ppermute | solution.py:768
  45.4 2.0 %collective-permute-start.3 = (f32[80,128]{1,0:T(8,128)}, f32[80,128]{1,0:T(8,128)S(1)}, u32[]{:S(2)}, u32[]{:S(2)}) collective-permute-start(f32[80,128]{1,0:T(8,128)} %get-tuple-element.40), channel_id=1, source_target_pairs={{64,0},{128,64},{192,128},{0,192},{65,1},{129,65},{193,129},{1,193... | collective-permute-start | bytes 122888 | tf_op jit(solution)/shard_map/ppermute | solution.py:768
  47.9 8.1 %contact.2 = (f32[64,128]{1,0:T(8,128)}, f32[64,128]{1,0:T(8,128)}) custom-call(s32[1,128]{1,0:T(1,128)} %refs_0_.7, f32[768,128]{1,0:T(8,128)} %bitcast.17, f32[768,128]{1,0:T(8,128)} %bitcast.18, f32[24,64]{1,0:T(8,128)} %get-tuple-element.32.refs_3_.refs_2_.refs_1_, f32[1,128]{1,0:T(1,128)} %convert_element_type.17.refs_4_.refs_5_, ...), custom_call_target="tpu_custom_call" | custom-call | bytes 33210000 | tf_op jit(solution)/shard_map/contact/pallas_call | solution.py:737
  56.0 5.1 %all-to-all-start.1 = ((f32[32,2,128]{2,1,0:T(2,128)}), f32[32,2,128]{2,1,0:T(2,128)S(1)}, u32[]{:S(2)}, u32[]{:S(2)}) async-start(f32[32,2,128]{2,1,0:T(2,128)} %bitcast.32), calls=%async_computation.1 | async-start | bytes 65536 | tf_op jit(solution)/shard_map/all_to_all | solution.py:758
  62.4 1.9 %faces_z.2 = (f32[16,128]{1,0:T(8,128)}, f32[16,128]{1,0:T(8,128)}) custom-call(f32[19,64,128]{2,1,0:T(8,128)} %get-tuple-element.36.refs_0_, f32[24,128]{1,0:T(8,128)} %copy-done.9, f32[24,128]{1,0:T(8,128)} %copy-done.10, f32[80,128]{1,0:T(8,128)} %copy-done.1, f32[80,128]{1,0:T(8,128)} %copy-done.2), custom_call_target="tpu_custom_call" | custom-call | bytes 7380000 | tf_op jit(solution)/shard_map/faces_z/pallas_call | solution.py:737
  66.0 2.6 %all-to-all-done.1 = f32[32,2,128]{2,1,0:T(2,128)S(1)} async-done(((f32[32,2,128]{2,1,0:T(2,128)}), f32[32,2,128]{2,1,0:T(2,128)S(1)}, u32[]{:S(2)}, u32[]{:S(2)}) %all-to-all-start.1) | async-done | bytes 32800 | tf_op jit(solution)/shard_map/all_to_all | solution.py:758
  69.8 2.0 %loads.2 = f32[64,128]{1,0:T(8,128)} custom-call(f32[64,128]{1,0:T(8,128)} %bitcast.28, f32[64,128]{1,0:T(8,128)} %get-tuple-element.35.refs_1_, f32[24,64]{1,0:T(8,128)} %get-tuple-element.32.refs_3_.refs_2_.refs_1_, f32[3,64,64]{2,1,0:T(8,128)} %refs_3_.7, f32[1,128]{1,0:T(1,128)} %convert_element_type.13.refs_6_.refs_4_.refs_2_, ...), custom_call_target="tpu_custom_call" | custom-call | bytes 7380000 | tf_op jit(solution)/shard_map/loads/pallas_call | solution.py:737
  71.8 6.1 %all-to-all-start.2 = ((f32[8,8,128]{2,1,0:T(8,128)}), f32[8,8,128]{2,1,0:T(8,128)S(1)}, u32[]{:S(2)}, u32[]{:S(2)}) async-start(f32[8,8,128]{2,1,0:T(8,128)} %bitcast.30), calls=%async_computation.2 | async-start | bytes 65536 | tf_op jit(solution)/shard_map/all_to_all | solution.py:758
  78.0 5.8 %stream_interp.1 = (f32[19,4,16,128]{3,2,1,0:T(8,128)}, f32[64,128]{1,0:T(8,128)}, f32[3,64,128]{2,1,0:T(8,128)}) custom-call(f32[19,64,128]{2,1,0:T(8,128)} %get-tuple-element.36.refs_0_, s32[4,16,128]{2,1,0:T(8,128)} %refs_1_.7, f32[768,128]{1,0:T(8,128)} %bitcast.19, f32[24,128]{1,0:T(8,128)} %copy-done.9, f32[24,128]{1,0:T(8,128)} %copy-done.10, ...), custom_call_target="tpu_custom_call" | custom-call | bytes 25830000 | tf_op jit(solution)/shard_map/stream_interp/pallas_call | solution.py:737
  87.2 15.1 %all_to_all.30 = f32[32,4,128]{2,1,0:T(4,128)} all-to-all(f32[32,4,128]{2,1,0:T(4,128)} %bitcast.31), channel_id=1, replica_groups=mesh['gx'=4,'gy'=8,'gz'=8] {'gx','gz'}, dimensions={0} | all-to-all | bytes 131072 | tf_op jit(solution)/shard_map/all_to_all | solution.py:758
  102.3 8.0 %contact.3 = (f32[64,128]{1,0:T(8,128)}, f32[64,128]{1,0:T(8,128)}) custom-call(s32[1,128]{1,0:T(1,128)} %refs_0_.7, f32[768,128]{1,0:T(8,128)} %bitcast.20, f32[128,128]{1,0:T(8,128)} %bitcast.22, f32[24,64]{1,0:T(8,128)} %get-tuple-element.53.refs_3_.refs_2_.refs_1_, f32[1,128]{1,0:T(1,128)} %convert_element_type.17.refs_4_.refs_5_, ...), custom_call_target="tpu_custom_call" | custom-call | bytes 33210000 | tf_op jit(solution)/shard_map/contact/pallas_call | solution.py:737
  110.3 3.9 %all-to-all-start.4 = ((f32[32,2,128]{2,1,0:T(2,128)}), f32[32,2,128]{2,1,0:T(2,128)S(1)}, u32[]{:S(2)}, u32[]{:S(2)}) async-start(f32[32,2,128]{2,1,0:T(2,128)} %bitcast.33), calls=%async_computation.4 | async-start | bytes 65536 | tf_op jit(solution)/shard_map/all_to_all | solution.py:758
  114.2 6.3 %fluid_two.1 = (f32[19,64,128]{2,1,0:T(8,128)}, f32[24,128]{1,0:T(8,128)}, f32[24,128]{1,0:T(8,128)}) custom-call(f32[768,128]{1,0:T(8,128)} %bitcast.21, f32[128,128]{1,0:T(8,128)} %bitcast.23, f32[19,4,16,128]{3,2,1,0:T(8,128)} %get-tuple-element.45.refs_2_, s32[4,16,128]{2,1,0:T(8,128)} %refs_1_.7, f32[3,64,128]{2,1,0:T(8,128)} %get-tuple-element.43.refs_5_.refs_4_), custom_call_target="tpu_custom_call" | custom-call | bytes 29520000 | tf_op jit(solution)/shard_map/fluid_two/pallas_call | solution.py:737
  120.8 2.4 %collective-permute-start.7 = (f32[24,128]{1,0:T(8,128)}, f32[24,128]{1,0:T(8,128)S(1)}, u32[]{:S(2)}, u32[]{:S(2)}) collective-permute-start(f32[24,128]{1,0:T(8,128)} %get-tuple-element.48), channel_id=1, source_target_pairs={{8,0},{16,8},{24,16},{32,24},{40,32},{48,40},{56,48},{0,56},{9,1},... | collective-permute-start | bytes 36872 | tf_op jit(solution)/shard_map/ppermute | solution.py:768
  123.8 2.0 %loads.3 = f32[64,128]{1,0:T(8,128)} custom-call(f32[64,128]{1,0:T(8,128)} %bitcast.29, f32[64,128]{1,0:T(8,128)} %get-tuple-element.56.refs_1_, f32[24,64]{1,0:T(8,128)} %get-tuple-element.53.refs_3_.refs_2_.refs_1_, f32[3,64,64]{2,1,0:T(8,128)} %refs_3_.7, f32[1,128]{1,0:T(1,128)} %convert_element_type.13.refs_6_.refs_4_.refs_2_, ...), custom_call_target="tpu_custom_call" | custom-call | bytes 7380000 | tf_op jit(solution)/shard_map/loads/pallas_call | solution.py:737
  125.8 4.9 %all-to-all-start.5 = ((f32[8,8,128]{2,1,0:T(8,128)}), f32[8,8,128]{2,1,0:T(8,128)S(1)}, u32[]{:S(2)}, u32[]{:S(2)}) async-start(f32[8,8,128]{2,1,0:T(8,128)} %bitcast.27), calls=%async_computation.5 | async-start | bytes 65536 | tf_op jit(solution)/shard_map/all_to_all | solution.py:758
  140.9 3.3 %collective-permute-start.10 = (f32[16,128]{1,0:T(8,128)}, f32[16,128]{1,0:T(8,128)S(1)}, u32[]{:S(2)}, u32[]{:S(2)}) collective-permute-start(f32[16,128]{1,0:T(8,128)} %get-tuple-element.51), channel_id=1, source_target_pairs={{0,1},{1,2},{2,3},{3,4},{4,5},{5,6},{6,7},{7,0},{8,9},{9,10},{10,1... | collective-permute-start | bytes 24584 | tf_op jit(solution)/shard_map/ppermute | solution.py:768
  145.1 2.3 %collective-permute-done.11.refs_7_ = f32[16,128]{1,0:T(8,128)S(1)} collective-permute-done((f32[16,128]{1,0:T(8,128)}, f32[16,128]{1,0:T(8,128)S(1)}, u32[]{:S(2)}, u32[]{:S(2)}) %collective-permute-start.11) | collective-permute-done | bytes 8224 | tf_op jit(solution)/shard_map/ppermute | solution.py:768
  148.0 2.3 %stream.1 = f32[19,4,16,128]{3,2,1,0:T(8,128)} custom-call(f32[19,64,128]{2,1,0:T(8,128)} %get-tuple-element.46.refs_0_, s32[4,16,128]{2,1,0:T(8,128)} %refs_1_.7, f32[24,128]{1,0:T(8,128)} %copy-done.11, f32[24,128]{1,0:T(8,128)} %copy-done.12, f32[80,128]{1,0:T(8,128)} %copy-done.3, f32[80,128]{1,0:T(8,128)} %copy-done.4, f32[16,128]{1,0:T(8,128)} %copy-done.15, ...), custom_call_target="tpu_custom_call" | custom-call | bytes 7380000 | tf_op jit(solution)/shard_map/stream/pallas_call | solution.py:737
  (68 shorter events, 32.5 us)
Async XLA Ops:
  6.4 18.7 %all-to-all-start = ((f32[32,24,128]{2,1,0:T(8,128)}), f32[32,24,128]{2,1,0:T(8,128)S(1)}, u32[]{:S(2)}, u32[]{:S(2)}) async-start(f32[32,24,128]{2,1,0:T(8,128)} %bitcast.24), calls=%async_computation | async-start | bytes 786432 | tf_op jit(solution)/shard_map/all_to_all | solution.py:758
  21.7 25.7 %copy-start.17 = (s32[1,128]{1,0:T(1,128)S(1)}, s32[1,128]{1,0:T(1,128)}, u32[]{:S(2)}) copy-start(s32[1,128]{1,0:T(1,128)} %refs_0_.7) | copy-start | bytes 1540
  25.2 0.8 copy-start
  35.5 6.9 %collective-permute-start = (f32[24,128]{1,0:T(8,128)}, f32[24,128]{1,0:T(8,128)S(1)}, u32[]{:S(2)}, u32[]{:S(2)}) collective-permute-start(f32[24,128]{1,0:T(8,128)} %get-tuple-element.37), channel_id=1, source_target_pairs={{0,8},{8,16},{16,24},{24,32},{32,40},{40,48},{48,56},{56,0},{1,9},... | collective-permute-start | bytes 36872 | tf_op jit(solution)/shard_map/ppermute | solution.py:768
  37.1 5.3 %collective-permute-start.1 = (f32[24,128]{1,0:T(8,128)}, f32[24,128]{1,0:T(8,128)S(1)}, u32[]{:S(2)}, u32[]{:S(2)}) collective-permute-start(f32[24,128]{1,0:T(8,128)} %get-tuple-element.38), channel_id=1, source_target_pairs={{8,0},{16,8},{24,16},{32,24},{40,32},{48,40},{56,48},{0,56},{9,1},... | collective-permute-start | bytes 36872 | tf_op jit(solution)/shard_map/ppermute | solution.py:768
  44.7 16.5 %collective-permute-start.2 = (f32[80,128]{1,0:T(8,128)}, f32[80,128]{1,0:T(8,128)S(1)}, u32[]{:S(2)}, u32[]{:S(2)}) collective-permute-start(f32[80,128]{1,0:T(8,128)} %get-tuple-element.39), channel_id=1, source_target_pairs={{0,64},{64,128},{128,192},{192,0},{1,65},{65,129},{129,193},{193,1... | collective-permute-start | bytes 122888 | tf_op jit(solution)/shard_map/ppermute | solution.py:768
  45.4 15.8 %collective-permute-start.3 = (f32[80,128]{1,0:T(8,128)}, f32[80,128]{1,0:T(8,128)S(1)}, u32[]{:S(2)}, u32[]{:S(2)}) collective-permute-start(f32[80,128]{1,0:T(8,128)} %get-tuple-element.40), channel_id=1, source_target_pairs={{64,0},{128,64},{192,128},{0,192},{65,1},{129,65},{193,129},{1,193... | collective-permute-start | bytes 122888 | tf_op jit(solution)/shard_map/ppermute | solution.py:768
  56.0 12.5 %all-to-all-start.1 = ((f32[32,2,128]{2,1,0:T(2,128)}), f32[32,2,128]{2,1,0:T(2,128)S(1)}, u32[]{:S(2)}, u32[]{:S(2)}) async-start(f32[32,2,128]{2,1,0:T(2,128)} %bitcast.32), calls=%async_computation.1 | async-start | bytes 65536 | tf_op jit(solution)/shard_map/all_to_all | solution.py:758
  61.8 0.6 copy-start.2
  64.3 4.2 %collective-permute-start.4 = (f32[16,128]{1,0:T(8,128)}, f32[16,128]{1,0:T(8,128)S(1)}, u32[]{:S(2)}, u32[]{:S(2)}) collective-permute-start(f32[16,128]{1,0:T(8,128)} %get-tuple-element.41), channel_id=1, source_target_pairs={{0,1},{1,2},{2,3},{3,4},{4,5},{5,6},{6,7},{7,0},{8,9},{9,10},{10,1... | collective-permute-start | bytes 24584 | tf_op jit(solution)/shard_map/ppermute | solution.py:768
  65.9 3.3 %collective-permute-start.5 = (f32[16,128]{1,0:T(8,128)}, f32[16,128]{1,0:T(8,128)S(1)}, u32[]{:S(2)}, u32[]{:S(2)}) collective-permute-start(f32[16,128]{1,0:T(8,128)} %get-tuple-element.42), channel_id=1, source_target_pairs={{1,0},{2,1},{3,2},{4,3},{5,4},{6,5},{7,6},{0,7},{9,8},{10,9},{11,1... | collective-permute-start | bytes 24584 | tf_op jit(solution)/shard_map/ppermute | solution.py:768
  68.5 0.7 copy-start.7
  68.5 0.7 copy-start.13
  71.8 13.0 %all-to-all-start.2 = ((f32[8,8,128]{2,1,0:T(8,128)}), f32[8,8,128]{2,1,0:T(8,128)S(1)}, u32[]{:S(2)}, u32[]{:S(2)}) async-start(f32[8,8,128]{2,1,0:T(8,128)} %bitcast.30), calls=%async_computation.2 | async-start | bytes 65536 | tf_op jit(solution)/shard_map/all_to_all | solution.py:758
  110.3 12.9 %all-to-all-start.4 = ((f32[32,2,128]{2,1,0:T(2,128)}), f32[32,2,128]{2,1,0:T(2,128)S(1)}, u32[]{:S(2)}, u32[]{:S(2)}) async-start(f32[32,2,128]{2,1,0:T(2,128)} %bitcast.33), calls=%async_computation.4 | async-start | bytes 65536 | tf_op jit(solution)/shard_map/all_to_all | solution.py:758
  120.5 10.2 %collective-permute-start.6 = (f32[24,128]{1,0:T(8,128)}, f32[24,128]{1,0:T(8,128)S(1)}, u32[]{:S(2)}, u32[]{:S(2)}) collective-permute-start(f32[24,128]{1,0:T(8,128)} %get-tuple-element.47), channel_id=1, source_target_pairs={{0,8},{8,16},{16,24},{24,32},{32,40},{40,48},{48,56},{56,0},{1,9},... | collective-permute-start | bytes 36872 | tf_op jit(solution)/shard_map/ppermute | solution.py:768
  120.8 9.9 %collective-permute-start.7 = (f32[24,128]{1,0:T(8,128)}, f32[24,128]{1,0:T(8,128)S(1)}, u32[]{:S(2)}, u32[]{:S(2)}) collective-permute-start(f32[24,128]{1,0:T(8,128)} %get-tuple-element.48), channel_id=1, source_target_pairs={{8,0},{16,8},{24,16},{32,24},{40,32},{48,40},{56,48},{0,56},{9,1},... | collective-permute-start | bytes 36872 | tf_op jit(solution)/shard_map/ppermute | solution.py:768
  125.8 24.5 %all-to-all-start.5 = ((f32[8,8,128]{2,1,0:T(8,128)}), f32[8,8,128]{2,1,0:T(8,128)S(1)}, u32[]{:S(2)}, u32[]{:S(2)}) async-start(f32[8,8,128]{2,1,0:T(8,128)} %bitcast.27), calls=%async_computation.5 | async-start | bytes 65536 | tf_op jit(solution)/shard_map/all_to_all | solution.py:758
  133.1 4.6 %collective-permute-start.8 = (f32[80,128]{1,0:T(8,128)}, f32[80,128]{1,0:T(8,128)S(1)}, u32[]{:S(2)}, u32[]{:S(2)}) collective-permute-start(f32[80,128]{1,0:T(8,128)} %get-tuple-element.49), channel_id=1, source_target_pairs={{0,64},{64,128},{128,192},{192,0},{1,65},{65,129},{129,193},{193,1... | collective-permute-start | bytes 122888 | tf_op jit(solution)/shard_map/ppermute | solution.py:768
  134.5 3.4 %collective-permute-start.9 = (f32[80,128]{1,0:T(8,128)}, f32[80,128]{1,0:T(8,128)S(1)}, u32[]{:S(2)}, u32[]{:S(2)}) collective-permute-start(f32[80,128]{1,0:T(8,128)} %get-tuple-element.50), channel_id=1, source_target_pairs={{64,0},{128,64},{192,128},{0,192},{65,1},{129,65},{193,129},{1,193... | collective-permute-start | bytes 122888 | tf_op jit(solution)/shard_map/ppermute | solution.py:768
  137.7 0.6 copy-start.3
  140.9 4.3 %collective-permute-start.10 = (f32[16,128]{1,0:T(8,128)}, f32[16,128]{1,0:T(8,128)S(1)}, u32[]{:S(2)}, u32[]{:S(2)}) collective-permute-start(f32[16,128]{1,0:T(8,128)} %get-tuple-element.51), channel_id=1, source_target_pairs={{0,1},{1,2},{2,3},{3,4},{4,5},{5,6},{6,7},{7,0},{8,9},{9,10},{10,1... | collective-permute-start | bytes 24584 | tf_op jit(solution)/shard_map/ppermute | solution.py:768
  144.1 3.3 %collective-permute-start.11 = (f32[16,128]{1,0:T(8,128)}, f32[16,128]{1,0:T(8,128)S(1)}, u32[]{:S(2)}, u32[]{:S(2)}) collective-permute-start(f32[16,128]{1,0:T(8,128)} %get-tuple-element.52), channel_id=1, source_target_pairs={{1,0},{2,1},{3,2},{4,3},{5,4},{6,5},{7,6},{0,7},{9,8},{10,9},{11,1... | collective-permute-start | bytes 24584 | tf_op jit(solution)/shard_map/ppermute | solution.py:768
  145.1 2.3 %copy-start.15 = (f32[16,128]{1,0:T(8,128)}, f32[16,128]{1,0:T(8,128)S(1)}, u32[]{:S(2)}) copy-start(f32[16,128]{1,0:T(8,128)S(1)} %collective-permute-done.10.refs_6_) | copy-start | bytes 24580
  (11 other events, 6.6 us)
